TPU v7x, 128 devices: a whole 4x4x4 slice. The times are simulated.
128 devices in a mesh: req: 8 (over y, core), exp: 16 (over z, x).
Axes of the slice: x: 4, y: 4, z: 4, core: 2. Of those that a mesh axis runs over, the one named last changes fastest.
Arguments:
- hidden: bfloat16 [16384, 2048], P(('req', 'exp')), may hold values from -6 to 6
- lengths: int32 [8, 4], P('req'), may hold values from 1 to 1536, 2048 in all within a row
- attn_gain: float32 [2048], replicated, may hold values from 0.25 to 1.75
- q_gain: float32 [128], replicated, may hold values from 1 to 4.5
- key_norm_gain: float32 [128], replicated, may hold values from 0.1 to 1.9
- w_query: bfloat16 [2048, 4096], P(None, 'exp'), may hold values from -0.125 to 0.125
- key_value_weight: bfloat16 [2048, 1024], replicated, may hold values from -0.125 to 0.125
- w_out: bfloat16 [4096, 2048], P('exp'), may hold values from -0.09375 to 0.09375
- ffn_gain: float32 [2048], replicated, may hold values from 0.25 to 1.75
- w_router: bfloat16 [2048, 128], replicated, may hold values from -0.125 to 0.125
- routes: int32 [16384, 8], P(('req', 'exp')), may hold values from 0 to 127, all different within a row; in each aligned block of 128 rows (0 to 127, 128 to 255, ...) at most 16 rows name the same one
- w_gate: bfloat16 [128, 2048, 768], P(('req', 'exp')), may hold values from -0.125 to 0.125
- w_up: bfloat16 [128, 2048, 768], P(('req', 'exp')), may hold values from -0.125 to 0.125
- w_down: bfloat16 [128, 768, 2048], P(('req', 'exp')), may hold values from -0.21875 to 0.21875
- page_table: int32 [1024], P(('req', 'exp')), may hold values from 0 to 1023, as said below
Outputs:
- layer_out: bfloat16 [16384, 2048], P(('req', 'exp'))
- kv_cache: bfloat16 [1024, 16384], P(('req', 'exp'))
Inputs may be any that keep to these rules, and one draw needn't show every extreme that they name: `routes`: in the rows of one device no expert is named more than 16 times. `page_table`: every page number appears exactly once. The blocks of the device with index (r, x) go to pages held by devices with exp index x, exactly (8) // 8 of them to each req index; the device with flat index i holds pages i * (8) onwards.
All inputs are finite; a program needn't handle non-finite values.
Results may differ from a plain program's by a relative error of at most 0.013.
Values may be sent and summed in bfloat16 or wider, within the bound.
A program may use at most 128 MiB of HBM per device.

v0:
```python
import math

import jax
import jax.numpy as jnp
from jax import lax
from jax.sharding import PartitionSpec as P

EPSILON = 1e-06
THETA_BASE = 1000000.0


def rms_norm(values, scale_gain):
    values = values.astype(jnp.float32)
    factor = lax.rsqrt(jnp.mean(values * values, -1, keepdims=True) + EPSILON)
    return values * factor * scale_gain


def rotate(values, positions):
    half_dim = values.shape[-1] // 2
    freqs = THETA_BASE ** (-jnp.arange(half_dim, dtype=jnp.float32) * 2.0 / values.shape[-1])
    angles = positions.astype(jnp.float32)[:, None] * freqs[None, :]
    cosine = jnp.cos(angles)[:, None, :]
    sine = jnp.sin(angles)[:, None, :]
    first_half = values[..., :half_dim]
    second_half = values[..., half_dim:]
    return jnp.concatenate(
        [first_half * cosine - second_half * sine, second_half * cosine + first_half * sine], -1
    )


def head_prepare(raw, scale_gain, positions, head_dim):
    row_count = raw.shape[0]
    split_heads = raw.reshape(row_count, raw.shape[1] // head_dim, head_dim)
    return (
        rotate(rms_norm(split_heads, scale_gain), positions)
        .reshape(row_count, raw.shape[1])
        .astype(jnp.bfloat16)
    )


def layout(prompt_lengths, row_count):
    ends = jnp.cumsum(prompt_lengths)
    starts = ends - prompt_lengths
    index = jnp.arange(row_count, dtype=jnp.int32)
    inside = (index[:, None] >= starts[None, :]) & (index[:, None] < ends[None, :])
    labels = jnp.arange(prompt_lengths.shape[0], dtype=jnp.int32)
    prompt = jnp.sum(jnp.where(inside, labels[None, :], 0), 1)
    token_position = index - jnp.sum(jnp.where(inside, starts[None, :], 0), 1)
    return (prompt, token_position)


def attend(query, key_rows, values_in, prompt, token_position, head_dim):
    row_count = query.shape[0]
    head_count = query.shape[1] // head_dim
    block_rows = min(512, row_count)
    block_list = row_count // block_rows
    query_blocks = query.reshape(block_list, block_rows, head_count, head_dim)

    def one_block(args):
        query_part, prompt_part, position_part = args
        scores = jnp.einsum(
            "qhd,kd->hqk", query_part, key_rows, preferred_element_type=jnp.float32
        ) / math.sqrt(head_dim)
        allowed = (prompt_part[:, None] == prompt[None, :]) & (
            token_position[None, :] <= position_part[:, None]
        )
        scores = jnp.where(allowed[None], scores, -1e30)
        highest = jnp.max(scores, -1, keepdims=True)
        weights = jnp.exp(scores - highest)
        soft = (weights / jnp.sum(weights, -1, keepdims=True)).astype(jnp.bfloat16)
        mixed = jnp.einsum("hqk,kd->qhd", soft, values_in, preferred_element_type=jnp.float32)
        return mixed.reshape(block_rows, head_count * head_dim).astype(jnp.bfloat16)

    result = lax.map(
        one_block,
        (
            query_blocks,
            prompt.reshape(block_list, block_rows),
            token_position.reshape(block_list, block_rows),
        ),
    )
    return result.reshape(row_count, head_count * head_dim)


def on_device(
    hidden,
    lengths,
    attn_gain,
    q_gain,
    key_norm_gain,
    w_query,
    key_value_weight,
    w_out,
    ffn_gain,
    w_router,
    routes,
    w_gate,
    w_up,
    w_down,
    page_table,
):
    head_dim = q_gain.shape[0]
    kv_heads = key_value_weight.shape[1] // (2 * head_dim)
    local_heads = w_query.shape[1] // head_dim
    query_heads = local_heads * lax.axis_size("exp")
    column = lax.axis_index("exp")
    tokens_here = hidden.shape[0]
    model_width = hidden.shape[1]
    group_rows = tokens_here * lax.axis_size("exp")
    normed = rms_norm(hidden, attn_gain).astype(jnp.bfloat16)
    prompt, token_position = layout(lengths[0], group_rows)
    own_position = lax.dynamic_slice_in_dim(token_position, column * tokens_here, tokens_here)
    key_value = jnp.dot(normed, key_value_weight, preferred_element_type=jnp.float32)
    own_keys = head_prepare(
        key_value[:, : kv_heads * head_dim], key_norm_gain, own_position, head_dim
    )
    own_rows = jnp.concatenate(
        [own_keys, key_value[:, kv_heads * head_dim :].astype(jnp.bfloat16)], 1
    )
    key_value_index = column * local_heads // (query_heads // kv_heads)
    key_cols = key_value_index * head_dim
    value_cols = key_cols + kv_heads * head_dim
    raw = jnp.dot(
        lax.all_gather(normed, "exp", axis=0, tiled=True),
        w_query,
        preferred_element_type=jnp.float32,
    )
    query = head_prepare(raw, q_gain, token_position, head_dim)
    every_row = lax.all_gather(own_rows, "exp", axis=0, tiled=True)
    key_rows = lax.dynamic_slice_in_dim(every_row, key_cols, head_dim, 1)
    value_rows_all = lax.dynamic_slice_in_dim(every_row, value_cols, head_dim, 1)
    mixed = attend(query, key_rows, value_rows_all, prompt, token_position, head_dim)
    projected = lax.psum_scatter(
        jnp.dot(mixed, w_out, preferred_element_type=jnp.float32).astype(jnp.bfloat16),
        "exp",
        scatter_dimension=0,
        tiled=True,
    ).astype(jnp.float32)
    resid = (hidden.astype(jnp.float32) + projected).astype(jnp.bfloat16)
    moe_in = rms_norm(resid, ffn_gain).astype(jnp.bfloat16)
    logits = jnp.dot(moe_in, w_router, preferred_element_type=jnp.float32)
    soft_router = jax.nn.softmax(logits, -1)
    expert_count = w_router.shape[1]
    top_count = routes.shape[1]
    chosen = routes[:, :, None] == jnp.arange(expert_count, dtype=jnp.int32)[None, None, :]
    picked = jnp.sum(jnp.where(chosen, soft_router[:, None, :], 0.0), -1)
    gates = picked / jnp.sum(picked, 1, keepdims=True)
    capacity = 2 * tokens_here * top_count // expert_count
    flat_chosen = chosen.reshape(tokens_here * top_count, expert_count).astype(jnp.int32)
    ranks = jnp.cumsum(flat_chosen, 0) - 1
    slot_ids = jnp.sum(ranks * flat_chosen, 1)
    target = routes.reshape(-1) * capacity + slot_ids
    source_rows = moe_in[jnp.arange(tokens_here * top_count, dtype=jnp.int32) // top_count]
    send_rows = (
        jnp.zeros((expert_count * capacity, model_width), jnp.bfloat16).at[target].set(source_rows)
    )
    direct = send_rows.reshape(expert_count, capacity, model_width)
    batch = lax.all_to_all(direct, ("req", "exp"), split_axis=0, concat_axis=0, tiled=True)
    batch_shape = batch.shape
    rows_flat = batch.reshape(-1, batch_shape[-1])
    gate_part = jnp.dot(rows_flat, w_gate[0], preferred_element_type=jnp.float32)
    up_part = jnp.dot(rows_flat, w_up[0], preferred_element_type=jnp.float32)
    act = (jax.nn.silu(gate_part) * up_part).astype(jnp.bfloat16)
    answer = jnp.dot(act, w_down[0], preferred_element_type=jnp.float32).astype(jnp.bfloat16)
    answered = answer.reshape(batch_shape[:-1] + (w_down.shape[2],))
    returned = lax.all_to_all(answered, ("req", "exp"), split_axis=0, concat_axis=0, tiled=True)
    outcome = returned.reshape(expert_count * capacity, model_width)[target]
    outcome = outcome.reshape(tokens_here, top_count, model_width)
    moe_sum = jnp.sum(outcome.astype(jnp.float32) * gates[:, :, None], 1)
    layer_out = (resid.astype(jnp.float32) + moe_sum).astype(jnp.bfloat16)
    blocks_here = page_table.shape[0]
    page_size = tokens_here // blocks_here
    page_width = page_size * own_rows.shape[1]
    page_blocks = own_rows.reshape(blocks_here, page_width)
    req_count = lax.axis_size("req")
    per_peer = blocks_here // req_count
    owner = page_table // blocks_here // lax.axis_size("exp")
    owner_hit = (owner[:, None] == jnp.arange(req_count, dtype=jnp.int32)[None, :]).astype(
        jnp.int32
    )
    rank_inside = jnp.sum((jnp.cumsum(owner_hit, 0) - 1) * owner_hit, 1)
    send_order = owner * per_peer + rank_inside
    send_pages = jnp.zeros_like(page_blocks).at[send_order].set(page_blocks)
    send_slots = jnp.zeros_like(page_table).at[send_order].set(page_table % blocks_here)
    got_pages, got_slots = (
        lax.all_to_all(
            send_pages.reshape(req_count, per_peer, page_width),
            "req",
            split_axis=0,
            concat_axis=0,
            tiled=True,
        ),
        lax.all_to_all(
            send_slots.reshape(req_count, per_peer), "req", split_axis=0, concat_axis=0, tiled=True
        ),
    )
    kv_cache = (
        jnp.zeros_like(page_blocks)
        .at[got_slots.reshape(-1)]
        .set(got_pages.reshape(blocks_here, page_width))
    )
    return (layer_out, kv_cache)


def solution(mesh):
    in_specs = (
        P(("req", "exp"), None),
        P("req", None),
        P(),
        P(),
        P(),
        P(None, "exp"),
        P(),
        P("exp", None),
        P(),
        P(),
        P(("req", "exp"), None),
        P(("req", "exp"), None, None),
        P(("req", "exp"), None, None),
        P(("req", "exp"), None, None),
        P(("req", "exp")),
    )
    out_specs = (P(("req", "exp"), None), P(("req", "exp"), None))
    return jax.shard_map(
        on_device, mesh=mesh, in_specs=in_specs, out_specs=out_specs, check_vma=False
    )
```

profile of v0, /device:TPU:13, one launch (start us, length us, event | category | flops | bytes accessed | tf_op | source)
XLA Modules:
  0.0 660.9 jit_solution(14308455975298828681)
XLA Ops:
  11.2 3.1 fusion.82
  23.6 6.3 multiply_cosine_fusion
  29.8 46.1 %all-gather.5.cloned.1.call-done = bf16[2048,1024]{1,0:T(8,128)(2,1)} async-done(((bf16[128,1024]{1,0:T(8,128)(2,1)}), bf16[2048,1024]{1,0:T(8,128)(2,1)}) %all-gather.5.cloned.1.call-update) | async-done | bytes 4194320 | tf_op jit(solution)/shard_map/all_gather | solution.py:129
  75.9 2.3 constant_dynamic-slice_fusion.2
  80.2 68.8 %all-gather.3.cloned.1.call-done = bf16[2048,2048]{1,0:T(8,128)(2,1)} async-done(((bf16[128,2048]{1,0:T(8,128)(2,1)}), bf16[2048,2048]{1,0:T(8,128)(2,1)}) %all-gather.3.cloned.1.call-update) | async-done | bytes 8388624 | tf_op jit(solution)/shard_map/all_gather | solution.py:124
  149.0 7.4 %multiply_reduce_fusion = (f32[2048,2]{0,1:T(2,128)S(1)}, f32[2048,256]{0,1:T(8,128)}) fusion(bf16[2048,2048]{1,0:T(8,128)(2,1)} %all-gather.3.cloned.1.call-done, bf16[2048,256]{1,0:T(8,128)(2,1)} %param.22), kind=kOutput, calls=%fused_computation.51 | convolution fusion | flops 2148528128 | bytes 11550720 | tf_op jit(solution)/shard_map/dot_general | solution.py:123
  156.4 2.9 copy.84
  159.4 2.1 multiply_multiply_fusion
  164.0 69.8 %while.10 = (s32[]{:T(128)}, bf16[4,512,256]{2,1,0:T(8,128)(2,1)}, s32[4,512]{1,0:T(4,128)S(1)}, s32[2048]{0:T(1024)S(1)}, s32[2048]{0:T(1024)S(1)}, /*index=5*/...) while((s32[]{:T(128)}, bf16[4,512,256]{2,1,0:T(8,128)(2,1)}, ...), condition=%wide.region_9.10_spmd, body=%wide.region_6.9_spmd.sunk | while | flops 1089603584 | bytes 21532792 | solution.py:74
  165.9 7.9 %fusion.101 = (f32[2,512]{1,0:T(2,128)S(1)}, f32[2,512,2048]{2,1,0:T(8,128)}) fusion(pred[512,2048]{1,0:T(8,128)(4,1)} %compare_and_fusion.2, bf16[2048,128]{1,0:T(8,128)(2,1)} %get-tuple-element.247, bf16[4,512,2,128]{3,1,0,2:T(8,128)(2,1)} %get-tuple-element.246, s32[]{:T(128)S(6)} %copy.117), kind=kOutput, calls=%fused_computation.146.clone.1 | convolution fusion | flops 545261568 | bytes 10227716 | tf_op jit(solution)/shard_map/while/body/eval_jaxpr/sub | solution.py:69
  173.7 5.7 fusion.102
  183.2 7.9 %fusion.101 = (f32[2,512]{1,0:T(2,128)S(1)}, f32[2,512,2048]{2,1,0:T(8,128)}) fusion(pred[512,2048]{1,0:T(8,128)(4,1)} %compare_and_fusion.2, bf16[2048,128]{1,0:T(8,128)(2,1)} %get-tuple-element.247, bf16[4,512,2,128]{3,1,0,2:T(8,128)(2,1)} %get-tuple-element.246, s32[]{:T(128)S(6)} %copy.117), kind=kOutput, calls=%fused_computation.146.clone.1 | convolution fusion | flops 545261568 | bytes 10227716 | tf_op jit(solution)/shard_map/while/body/eval_jaxpr/sub | solution.py:69
  191.1 5.7 fusion.102
  200.5 7.9 %fusion.101 = (f32[2,512]{1,0:T(2,128)S(1)}, f32[2,512,2048]{2,1,0:T(8,128)}) fusion(pred[512,2048]{1,0:T(8,128)(4,1)} %compare_and_fusion.2, bf16[2048,128]{1,0:T(8,128)(2,1)} %get-tuple-element.247, bf16[4,512,2,128]{3,1,0,2:T(8,128)(2,1)} %get-tuple-element.246, s32[]{:T(128)S(6)} %copy.117), kind=kOutput, calls=%fused_computation.146.clone.1 | convolution fusion | flops 545261568 | bytes 10227716 | tf_op jit(solution)/shard_map/while/body/eval_jaxpr/sub | solution.py:69
  208.4 5.7 fusion.102
  217.9 7.9 %fusion.101 = (f32[2,512]{1,0:T(2,128)S(1)}, f32[2,512,2048]{2,1,0:T(8,128)}) fusion(pred[512,2048]{1,0:T(8,128)(4,1)} %compare_and_fusion.2, bf16[2048,128]{1,0:T(8,128)(2,1)} %get-tuple-element.247, bf16[4,512,2,128]{3,1,0,2:T(8,128)(2,1)} %get-tuple-element.246, s32[]{:T(128)S(6)} %copy.117), kind=kOutput, calls=%fused_computation.146.clone.1 | convolution fusion | flops 545261568 | bytes 10227716 | tf_op jit(solution)/shard_map/while/body/eval_jaxpr/sub | solution.py:69
  225.7 5.7 fusion.102
  233.7 7.1 %convolution_convert_fusion.1 = bf16[2048,2048]{1,0:T(8,128)(2,1)} fusion(bf16[2048,256]{1,0:T(8,128)(2,1)} %bitcast.130, bf16[256,2048]{1,0:T(8,128)(2,1)} %param.24), kind=kOutput, calls=%fused_computation.38 | convolution fusion | flops 2151677952 | bytes 10485760 | tf_op jit(solution)/shard_map/dot_general | solution.py:134
  244.8 79.1 %reduce-scatter.2.cloned.1.call-done = bf16[128,2048]{1,0:T(8,128)(2,1)} async-done(((bf16[2048,2048]{1,0:T(8,128)(2,1)}), bf16[128,2048]{1,0:T(8,128)(2,1)}) %reduce-scatter.2.cloned.1.call-update) | async-done | bytes 524304 | tf_op jit(solution)/shard_map/reduce_scatter | solution.py:133
  325.4 2.2 fusion.50
  327.6 25.1 %scatter_custom_fusion = bf16[2048,2048]{1,0:T(8,128)(2,1)} fusion(s32[1024]{0:T(1024)S(1)} %bitcast.138, bf16[128,2048]{1,0:T(8,128)(2,1)} %fusion.50, s32[1024]{0:T(1024)S(1)} %broadcast_clamp_fusion.1, bf16[]{:T(256)} %constant.128.clone.1), kind=kCustom, calls=%fused_computation.40 | custom fusion | bytes 8389120 | tf_op jit(solution)/shard_map/scatter | solution.py:155
  352.6 10.2 %all-to-all-start = ((bf16[128,16,2048]{2,1,0:T(8,128)(2,1)}), bf16[128,16,2048]{2,1,0:T(8,128)(2,1)}, u32[]{:S(2)}, u32[]{:S(2)}) async-start(bf16[128,16,2048]{2,1,0:T(8,128)(2,1)} %bitcast.126), calls=%async_computation.1 | async-start | bytes 16777216 | tf_op jit(solution)/shard_map/all_to_all | solution.py:158
  370.6 101.3 %all-to-all-done = bf16[128,16,2048]{2,1,0:T(8,128)(2,1)} async-done(((bf16[128,16,2048]{2,1,0:T(8,128)(2,1)}), bf16[128,16,2048]{2,1,0:T(8,128)(2,1)}, u32[]{:S(2)}, u32[]{:S(2)}) %all-to-all-start) | async-done | bytes 8388640 | tf_op jit(solution)/shard_map/all_to_all | solution.py:158
  472.0 4.3 all-to-all-start.2
  476.2 11.7 %fusion.41 = f32[2048,768]{1,0:T(8,128)} fusion(bf16[2048,2048]{1,0:T(8,128)(2,1)} %bitcast.22, bf16[1,2048,768]{2,1,0:T(8,128)(2,1)} %param.28), kind=kOutput, calls=%fused_computation.45 | convolution fusion | flops 6442450944 | bytes 17825792 | tf_op jit(solution)/shard_map/dot_general | solution.py:161
  487.9 4.8 all-to-all-start.3
  492.8 21.3 %convolution_convert_fusion = bf16[2048,2048]{1,0:T(8,128)(2,1)} fusion(f32[2048,768]{1,0:T(8,128)} %fusion.41, bf16[2048,2048]{1,0:T(8,128)(2,1)} %bitcast.22, bf16[1,768,2048]{2,1,0:T(8,128)(2,1)S(1)} %copy-done, bf16[1,2048,768]{2,1,0:T(8,128)(2,1)} %param.29), kind=kOutput, calls=%fused_computation.37 | convolution fusion | flops 12898533376 | bytes 29360128 | tf_op jit(solution)/shard_map/dot_general | solution.py:164
  514.0 10.1 %all-to-all-start.1 = ((bf16[128,16,2048]{2,1,0:T(8,128)(2,1)}), bf16[128,16,2048]{2,1,0:T(8,128)(2,1)}, u32[]{:S(2)}, u32[]{:S(2)}) async-start(bf16[128,16,2048]{2,1,0:T(8,128)(2,1)} %bitcast.127), calls=%async_computation.2 | async-start | bytes 16777216 | tf_op jit(solution)/shard_map/all_to_all | solution.py:166
  525.4 2.6 scatter_custom_fusion.3
  531.8 101.5 %all-to-all-done.1 = bf16[128,16,2048]{2,1,0:T(8,128)(2,1)} async-done(((bf16[128,16,2048]{2,1,0:T(8,128)(2,1)}), bf16[128,16,2048]{2,1,0:T(8,128)(2,1)}, u32[]{:S(2)}, u32[]{:S(2)}) %all-to-all-start.1) | async-done | bytes 8388640 | tf_op jit(solution)/shard_map/all_to_all | solution.py:166
  633.3 13.3 %gather_fusion = bf16[1024,2048]{1,0:T(8,128)(2,1)} fusion(bf16[2048,2048]{1,0:T(8,128)(2,1)} %bitcast.27, s32[1024]{0:T(1024)S(1)} %broadcast_clamp_fusion), kind=kCustom, calls=%fused_computation.1 | custom fusion | bytes 8392704 | tf_op jit(solution)/shard_map/gather | solution.py:167
  646.6 6.6 fusion.34
  (120 shorter events, 51.7 us)
Async XLA Ops:
  7.2 485.6 %copy-start = (bf16[1,768,2048]{2,1,0:T(8,128)(2,1)S(1)}, bf16[1,768,2048]{2,1,0:T(8,128)(2,1)}, u32[]{:S(2)}) copy-start(bf16[1,768,2048]{2,1,0:T(8,128)(2,1)} %param.30) | copy-start | bytes 9437188
  7.2 7.8 %copy-start.11 = (s32[1,4]{1,0:T(1,128)S(1)}, s32[1,4]{1,0:T(1,128)}, u32[]{:S(2)}) copy-start(s32[1,4]{1,0:T(1,128)} %param.18) | copy-start | bytes 52
  7.2 68.7 %all-gather.5.cloned.1.call-start = ((), (), s32[]{:S(2)}) async-start(), calls=%async_computation.6 | async-start | bytes 4456448 | tf_op jit(solution)/shard_map/all_gather | solution.py:129
  15.3 0.6 copy-start.7
  21.8 127.2 %all-gather.3.cloned.1.call-start = ((), (), s32[]{:S(2)}) async-start(), calls=%async_computation.5 | async-start | bytes 8912896 | tf_op jit(solution)/shard_map/all_gather | solution.py:124
  22.6 301.3 %reduce-scatter.2.cloned.1.call-start = ((), (), s32[]{:S(2)}) async-start(), calls=%async_computation.7 | async-start | bytes 8912896 | tf_op jit(solution)/shard_map/reduce_scatter | solution.py:133
  156.4 3.0 copy-start.10
  159.4 2.1 copy-start.3
  159.4 2.2 copy-start.4
  240.8 0.7 copy-start.8
  241.5 83.9 %copy-start.9 = (f32[2048]{0:T(1024)S(1)}, f32[2048]{0:T(1024)}, u32[]{:S(2)}) copy-start(f32[2048]{0:T(1024)} %param.25) | copy-start | bytes 24580
  242.3 0.8 copy-start.6
  352.6 10.2 %copy-start.5 = (bf16[128,1024]{1,0:T(8,128)(2,1)S(1)}, bf16[128,1024]{1,0:T(8,128)(2,1)}, u32[]{:S(2)}) copy-start(bf16[128,1024]{1,0:T(8,128)(2,1)} %pad_maximum_fusion.1) | copy-start | bytes 786436
  352.6 11.0 %copy-start.12 = (s32[8]{0:T(128)S(1)}, s32[8]{0:T(128)}, u32[]{:S(2)}) copy-start(s32[8]{0:T(128)} %param.31) | copy-start | bytes 100
  352.6 119.3 %all-to-all-start = ((bf16[128,16,2048]{2,1,0:T(8,128)(2,1)}), bf16[128,16,2048]{2,1,0:T(8,128)(2,1)}, u32[]{:S(2)}, u32[]{:S(2)}) async-start(bf16[128,16,2048]{2,1,0:T(8,128)(2,1)} %bitcast.126), calls=%async_computation.1 | async-start | bytes 16777216 | tf_op jit(solution)/shard_map/all_to_all | solution.py:158
  472.0 16.0 %all-to-all-start.2 = ((s32[8,1,1]{2,1,0:T(1,128)}), s32[8,1,1]{2,1,0:T(1,128)S(1)}, u32[]{:S(2)}, u32[]{:S(2)}) async-start(s32[8,1,1]{2,1,0:T(1,128)} %copy.97), calls=%async_computation.3 | async-start | bytes 8192 | tf_op jit(solution)/shard_map/all_to_all | solution.py:193
  487.9 26.1 %all-to-all-start.3 = ((bf16[8,2,8192]{2,1,0:T(2,128)(2,1)}), bf16[8,2,8192]{2,1,0:T(2,128)(2,1)S(1)}, u32[]{:S(2)}, u32[]{:S(2)}) async-start(bf16[8,2,8192]{2,1,0:T(2,128)(2,1)} %reshape.501), calls=%async_computation.4 | async-start | bytes 524288 | tf_op jit(solution)/shard_map/all_to_all | solution.py:186
  514.0 119.3 %all-to-all-start.1 = ((bf16[128,16,2048]{2,1,0:T(8,128)(2,1)}), bf16[128,16,2048]{2,1,0:T(8,128)(2,1)}, u32[]{:S(2)}, u32[]{:S(2)}) async-start(bf16[128,16,2048]{2,1,0:T(8,128)(2,1)} %bitcast.127), calls=%async_computation.2 | async-start | bytes 16777216 | tf_op jit(solution)/shard_map/all_to_all | solution.py:166
  646.6 6.6 %copy-start.1 = (bf16[128,2048]{1,0:T(8,128)(2,1)S(1)}, bf16[128,2048]{1,0:T(8,128)(2,1)}, u32[]{:S(2)}) copy-start(bf16[128,2048]{1,0:T(8,128)(2,1)} %param.17) | copy-start | bytes 1572868
  646.6 6.6 %copy-start.2 = (bf16[128,2048]{1,0:T(8,128)(2,1)S(1)}, bf16[128,2048]{1,0:T(8,128)(2,1)}, u32[]{:S(2)}) copy-start(bf16[128,2048]{1,0:T(8,128)(2,1)} %reduce-scatter.2.cloned.1.call-done) | copy-start | bytes 1572868
Sparse Core Ops, SparseCore 0:
  21.9 53.9 all-gather.4
  78.6 70.3 all-gather.2
  241.0 82.8 reduce-scatter.1
where the time goes:
time: 666 us; the launch traced here: 661 us
  waiting for transfers between devices  398 us (60%)
  matrix products  106 us (16%)
  local copies, waits for them, and re-layouts  68 us (10%)
  other arithmetic  44.4 us (7%)
  starting transfers between devices  29.7 us (4%)
  between operations  14.3 us (2%)
    all_to_all x1, waiting for transfers between devices, on_device(): lax.all_to_all(answered, ('req', 'exp'), split_axis=0, concat_axis=0, til...  101 us
    all_to_all x1, waiting for transfers between devices, on_device(): lax.all_to_all(direct, ('req', 'exp'), split_axis=0, concat_axis=0, tiled...  101 us
    reduce_scatter x1, waiting for transfers between devices, on_device(): lax.psum_scatter(jnp.dot(mixed, w_out, preferred_element_type=jnp.float32...  79.1 us
    all_gather x1, waiting for transfers between devices, on_device(): lax.all_gather(normed, 'exp', axis=0, tiled=True)  68.8 us
    all_gather x1, waiting for transfers between devices, on_device(): every_row = lax.all_gather(own_rows, 'exp', axis=0, tiled=True)  46.1 us
    sub x4, matrix products, one_block(): weights = jnp.exp(scores - highest)  31.5 us
    scatter x1, local copies, waits for them, and re-layouts, on_device(): jnp.zeros((expert_count * capacity, model_width), jnp.bfloat16).at[target]  25.1 us
    dot_general x4, matrix products, one_block(): jnp.einsum('hqk,kd->qhd', soft, values_in, preferred_element_type=jnp.flo...  22.9 us
  transfers between devices with their start and end apart: 7, of which 5 were waited for; matrix products, arithmetic and copies ran while one was open for 9% of the time, Pallas kernels for 0%

commit v1 on v0

v1 whole, which is shorter than its diff:
```python
import functools
import math

import jax
import jax.numpy as jnp
from jax import lax
from jax.experimental import pallas as pl
from jax.experimental.pallas import tpu as pltpu
from jax.sharding import PartitionSpec as P

EPSILON = 1e-06
THETA_BASE = 1000000.0
MESH = pl.DeviceIdType.MESH
BF = jnp.bfloat16
F32 = jnp.float32


def rms_norm(values, scale_gain):
    values = values.astype(jnp.float32)
    factor = lax.rsqrt(jnp.mean(values * values, -1, keepdims=True) + EPSILON)
    return values * factor * scale_gain


def head_norm_rope(raw, gain, cosf, sinf):
    factor = lax.rsqrt(jnp.mean(raw * raw, -1, keepdims=True) + EPSILON)
    y = raw * factor * gain
    return y * cosf + pltpu.roll(y, 64, 1) * sinf


def attention_kernel(
    normed, hidden, wq, kvw, wo, q_gain, k_gain, ffn_gain, cosf, sinf, start,
    resid_o, moe_o, rows_o,
    tok, wqa, kvv, woa, ka, va, qs, ss, peak, acc, mixed, rs, part,
    lsem, tsend, trecv, wsend, wrecv, osend, orecv, ksend, krecv, rsend, rrecv,
):
    req = lax.axis_index("req")
    col = lax.axis_index("exp")
    z = col // 4
    x = col % 4
    core = req % 2

    def dz(d):
        return (req, lax.rem(z + d, 4) * 4 + x)

    def dx(d):
        return (req, z * 4 + lax.rem(x + d, 4))

    partner = (req + 1 - 2 * core, col)
    z1, z2, z3 = lax.rem(z + 1, 4), lax.rem(z + 2, 4), lax.rem(z + 3, 4)
    x1, x2, x3 = lax.rem(x + 1, 4), lax.rem(x + 2, 4), lax.rem(x + 3, 4)
    sent = []

    def orow(xx, off, size):
        return pl.ds(pl.multiple_of(xx * 256 + off, 64), size)

    def send(src, dst, ssem, rsem, dev):
        c = pltpu.make_async_remote_copy(
            src_ref=src, dst_ref=dst, send_sem=ssem, recv_sem=rsem,
            device_id=dev, device_id_type=MESH,
        )
        c.start()
        sent.append(c)

    def got(dst, rsem, ssem):
        pltpu.make_async_remote_copy(
            src_ref=dst, dst_ref=dst, send_sem=ssem, recv_sem=rsem,
            device_id=partner, device_id_type=MESH,
        ).wait_recv()

    local_kv = pltpu.make_async_copy(kvw, kvv, lsem.at[0])
    local_kv.start()
    local_wq = pltpu.make_async_copy(wq, wqa.at[x], lsem.at[1])
    local_wq.start()
    local_wo = pltpu.make_async_copy(wo, woa.at[orow(x, 0, 256)], lsem.at[2])
    local_wo.start()
    tok[z] = normed[...]
    va[:, 128:256] = jnp.ones((2048, 128), BF)

    barrier = pltpu.get_barrier_semaphore()
    for dev in (dz(1), dz(2), dz(3), dx(1), dx(3), partner):
        pl.semaphore_signal(barrier, inc=1, device_id=dev, device_id_type=MESH)
    pl.semaphore_wait(barrier, 6)

    send(normed, tok.at[z], tsend.at[0], trecv.at[0], dz(1))
    send(normed, tok.at[z], tsend.at[1], trecv.at[1], dz(3))
    half = core * 1024
    send(wq.at[pl.ds(half, 1024)], wqa.at[x, pl.ds(half, 1024)], wsend.at[0], wrecv.at[0], dx(1))
    send(wq.at[pl.ds(half, 1024)], wqa.at[x, pl.ds(half, 1024)], wsend.at[1], wrecv.at[1], dx(3))

    def krow(zz, xx):
        return pl.ds(pl.multiple_of((zz * 4 + xx) * 128, 128), 128)

    def send_kv(zz, j):
        rows = krow(zz, x)
        k = ka.at[rows]
        v = va.at[rows, pl.ds(0, 128)]
        send(k, k, ksend.at[j, 0], krecv.at[j, 0], dx(1))
        send(v, v, ksend.at[j, 1], krecv.at[j, 1], dx(1))
        send(k, k, ksend.at[j, 2], krecv.at[j, 2], dx(3))
        send(v, v, ksend.at[j, 3], krecv.at[j, 3], dx(3))

    def relay_kv(zz, j):
        left = krow(zz, x3)
        right = krow(zz, x1)
        k = ka.at[left]
        got(k, krecv.at[j, 0], ksend.at[j, 0])
        send(k, k, ksend.at[j, 4], krecv.at[j, 4], dx(1))
        v = va.at[right, pl.ds(0, 128)]
        got(v, krecv.at[j, 3], ksend.at[j, 3])
        send(v, v, ksend.at[j, 5], krecv.at[j, 5], dx(3))

    def finish_kv(zz, j):
        left = krow(zz, x3)
        right = krow(zz, x1)
        far = krow(zz, x2)
        got(va.at[left, pl.ds(0, 128)], krecv.at[j, 1], ksend.at[j, 1])
        got(ka.at[right], krecv.at[j, 2], ksend.at[j, 2])
        got(ka.at[far], krecv.at[j, 4], ksend.at[j, 4])
        got(va.at[far, pl.ds(0, 128)], krecv.at[j, 5], ksend.at[j, 5])

    local_kv.wait()
    own = jnp.dot(normed[...], kvv[...], preferred_element_type=F32)
    for h in range(4):
        rows_o[:, h * 128 : (h + 1) * 128] = head_norm_rope(
            own[:, h * 128 : (h + 1) * 128], k_gain[...], cosf[z], sinf[z]
        ).astype(BF)
    rows_o[:, 512:1024] = own[:, 512:1024].astype(BF)
    kcols = pl.ds(pl.multiple_of(z * 128, 128), 128)
    vcols = pl.ds(pl.multiple_of(512 + z * 128, 128), 128)
    ka[krow(z, x), :] = rows_o[:, kcols]
    va[krow(z, x), 0:128] = rows_o[:, vcols]
    send_kv(z, 0)

    def make_kv(zz):
        block = tok[zz]
        kk = jnp.dot(block, kvv[:, kcols], preferred_element_type=F32)
        vv = jnp.dot(block, kvv[:, vcols], preferred_element_type=F32)
        ka[krow(zz, x), :] = head_norm_rope(kk, k_gain[...], cosf[zz], sinf[zz]).astype(BF)
        va[krow(zz, x), 0:128] = vv.astype(BF)

    got(tok.at[z3], trecv.at[0], tsend.at[0])
    send(tok.at[z3, pl.ds(0, 64)], tok.at[z3, pl.ds(0, 64)], tsend.at[2], trecv.at[2], dz(1))
    got(tok.at[z1], trecv.at[1], tsend.at[1])
    send(tok.at[z1, pl.ds(64, 64)], tok.at[z1, pl.ds(64, 64)], tsend.at[3], trecv.at[3], dz(3))
    mine = pl.ds(half, 1024)
    got(wqa.at[x3, mine], wrecv.at[0], wsend.at[0])
    r0 = wqa.at[x3, pl.ds(half, 512)]
    send(r0, r0, wsend.at[2], wrecv.at[2], dx(1))
    got(wqa.at[x1, mine], wrecv.at[1], wsend.at[1])
    r1 = wqa.at[x1, pl.ds(half + 512, 512)]
    send(r1, r1, wsend.at[3], wrecv.at[3], dx(3))
    p0 = wqa.at[x3, mine]
    send(p0, p0, wsend.at[4], wrecv.at[4], partner)
    p1 = wqa.at[x1, mine]
    send(p1, p1, wsend.at[5], wrecv.at[5], partner)

    make_kv(z3)
    send_kv(z3, 1)
    make_kv(z1)
    send_kv(z1, 2)
    relay_kv(z, 0)
    ohalf = core * 128
    omine = pl.ds(ohalf, 128)
    send(wo.at[omine], woa.at[orow(x, ohalf, 128)], osend.at[0], orecv.at[0], dx(1))
    send(wo.at[omine], woa.at[orow(x, ohalf, 128)], osend.at[1], orecv.at[1], dx(3))
    got(tok.at[z2, pl.ds(0, 64)], trecv.at[2], tsend.at[2])
    got(tok.at[z2, pl.ds(64, 64)], trecv.at[3], tsend.at[3])
    make_kv(z2)
    send_kv(z2, 3)
    relay_kv(z3, 1)
    relay_kv(z1, 2)

    got(wqa.at[x2, pl.ds(half, 512)], wrecv.at[2], wsend.at[2])
    got(wqa.at[x2, pl.ds(half + 512, 512)], wrecv.at[3], wsend.at[3])
    p2 = wqa.at[x2, mine]
    send(p2, p2, wsend.at[6], wrecv.at[6], partner)
    local_wq.wait()

    def q_slice(xx):
        for zz in range(2):
            block = jnp.concatenate([tok[2 * zz], tok[2 * zz + 1]], 0)
            raw = jnp.dot(block, wqa[xx], preferred_element_type=F32)
            for b in range(2):
                for h in range(2):
                    y = head_norm_rope(
                        raw[b * 128 : (b + 1) * 128, h * 128 : (h + 1) * 128],
                        q_gain[...], cosf[2 * zz + b], sinf[2 * zz + b],
                    )
                    row = pl.ds(pl.multiple_of((xx * 2 + h) * 128, 128), 128)
                    qs[2 * zz + b, row, :] = y.astype(BF)

    q_slice(x)
    other = pl.ds(1024 - half, 1024)
    got(wqa.at[x3, other], wrecv.at[4], wsend.at[4])
    q_slice(x3)
    relay_kv(z2, 3)
    got(wqa.at[x1, other], wrecv.at[5], wsend.at[5])
    q_slice(x1)
    got(wqa.at[x2, other], wrecv.at[6], wsend.at[6])
    q_slice(x2)

    left_o = woa.at[orow(x3, ohalf, 128)]
    right_o = woa.at[orow(x1, ohalf, 128)]
    far_o = woa.at[orow(x2, ohalf, 128)]
    got(left_o, orecv.at[0], osend.at[0])
    o0 = woa.at[orow(x3, ohalf, 64)]
    send(o0, o0, osend.at[2], orecv.at[2], dx(1))
    got(right_o, orecv.at[1], osend.at[1])
    o1 = woa.at[orow(x1, ohalf + 64, 64)]
    send(o1, o1, osend.at[3], orecv.at[3], dx(3))
    send(left_o, left_o, osend.at[4], orecv.at[4], partner)
    send(right_o, right_o, osend.at[5], orecv.at[5], partner)
    for zz, j in ((z, 0), (z3, 1), (z1, 2), (z2, 3)):
        finish_kv(zz, j)
    last_o = pltpu.make_async_remote_copy(
        src_ref=far_o, dst_ref=far_o, send_sem=osend.at[6], recv_sem=orecv.at[6],
        device_id=partner, device_id_type=MESH,
    )

    def attend(b):
        low = start[b]
        here = (b * 4 + x) * 128 + lax.broadcasted_iota(jnp.int32, (128, 512), 0)
        peak[...] = jnp.full((1024, 128), -1e30, F32)

        def score_step(c, carry):
            keys = pl.ds(pl.multiple_of(c * 512, 512), 512)
            s = lax.dot_general(
                qs[b], ka[keys, :], (((1,), (1,)), ((), ())), preferred_element_type=F32
            )
            kid = c * 512 + lax.broadcasted_iota(jnp.int32, (128, 512), 1)
            bias = jnp.where((kid >= low) & (kid <= here), 0.0, -1e30)
            s = (s.reshape(8, 128, 512) + bias[None]).reshape(1024, 512)
            ss[:, keys] = s
            top = peak[...]
            for g in range(4):
                top = jnp.maximum(top, s[:, g * 128 : (g + 1) * 128])
            peak[...] = top
            return carry

        lax.fori_loop(0, b + 1, score_step, 0)
        peak[...] = jnp.broadcast_to(jnp.max(peak[...], -1, keepdims=True), (1024, 128))
        acc[...] = jnp.zeros((1024, 256), F32)

        def mix_step(c, carry):
            keys = pl.ds(pl.multiple_of(c * 512, 512), 512)
            p = jnp.exp2(ss[:, keys] - peak[:, 0:1]).astype(BF)
            acc[...] += jnp.dot(p, va[keys, :], preferred_element_type=F32)
            return carry

        lax.fori_loop(0, b + 1, mix_step, 0)
        for h in range(8):
            rows = slice(h * 128, (h + 1) * 128)
            mixed[:, h * 128 : (h + 1) * 128] = (acc[rows, 0:128] / acc[rows, 128:256]).astype(BF)

    def share(i, off):
        b = lax.rem(z + off, 4)
        return pltpu.make_async_remote_copy(
            src_ref=part.at[b], dst_ref=rs.at[z], send_sem=rsend.at[i], recv_sem=rrecv.at[i],
            device_id=(req, b * 4 + x), device_id_type=MESH,
        )

    def block_step(i, carry):
        off = jnp.where(i == 0, 2, jnp.where(i == 1, 1, jnp.where(i == 2, 3, 0)))
        b = lax.rem(z + off, 4)
        attend(b)

        @pl.when(i == 0)
        def _():
            got(woa.at[orow(x2, ohalf, 64)], orecv.at[2], osend.at[2])
            got(woa.at[orow(x2, ohalf + 64, 64)], orecv.at[3], osend.at[3])
            last_o.start()
            got(woa.at[orow(x3, 128 - ohalf, 128)], orecv.at[4], osend.at[4])
            got(woa.at[orow(x1, 128 - ohalf, 128)], orecv.at[5], osend.at[5])
            got(woa.at[orow(x2, 128 - ohalf, 128)], orecv.at[6], osend.at[6])
            local_wo.wait()

        for n in range(2):
            cols = slice(n * 1024, (n + 1) * 1024)
            part[b, :, cols] = jnp.dot(
                mixed[...], woa[:, cols], preferred_element_type=F32
            ).astype(BF)

        @pl.when(i < 3)
        def _():
            share(i, off).start()

        return carry

    lax.fori_loop(0, 4, block_step, 0)
    for i, off in enumerate((2, 1, 3)):
        src = lax.rem(z + 4 - off, 4)
        got(rs.at[src], rrecv.at[i], rsend.at[i])
    total = hidden[...].astype(F32) + part[z].astype(F32)
    for d in range(1, 4):
        total = total + rs[lax.rem(z + d, 4)].astype(F32)
    resid = total.astype(BF)
    resid_o[...] = resid
    rf = resid.astype(F32)
    factor = lax.rsqrt(jnp.mean(rf * rf, -1, keepdims=True) + EPSILON)
    moe_o[...] = (rf * factor * ffn_gain[...]).astype(BF)
    for c in sent:
        c.wait_send()
    last_o.wait_send()
    for i, off in enumerate((2, 1, 3)):
        share(i, off).wait_send()


def attention_phase(normed, hidden, w_query, key_value_weight, w_out, q_gain, k_gain, ffn_gain, cosf, sinf, start):
    vmem = pl.BlockSpec(memory_space=pltpu.VMEM)
    hbm = pl.BlockSpec(memory_space=pl.ANY)
    dma = pltpu.SemaphoreType.DMA
    return pl.pallas_call(
        attention_kernel,
        name="attention",
        out_shape=(
            jax.ShapeDtypeStruct((128, 2048), BF),
            jax.ShapeDtypeStruct((128, 2048), BF),
            jax.ShapeDtypeStruct((128, 1024), BF),
        ),
        in_specs=[vmem, vmem, hbm, hbm, hbm, vmem, vmem, vmem, vmem, vmem, vmem],
        out_specs=(vmem, vmem, vmem),
        scratch_shapes=[
            pltpu.VMEM((4, 128, 2048), BF),
            pltpu.VMEM((4, 2048, 256), BF),
            pltpu.VMEM((2048, 1024), BF),
            pltpu.VMEM((1024, 2048), BF),
            pltpu.VMEM((2048, 128), BF),
            pltpu.VMEM((2048, 256), BF),
            pltpu.VMEM((4, 1024, 128), BF),
            pltpu.VMEM((1024, 2048), F32),
            pltpu.VMEM((1024, 128), F32),
            pltpu.VMEM((1024, 256), F32),
            pltpu.VMEM((128, 1024), BF),
            pltpu.VMEM((4, 128, 2048), BF),
            pltpu.VMEM((4, 128, 2048), BF),
            dma((3,)), dma((4,)), dma((4,)), dma((7,)), dma((7,)), dma((7,)), dma((7,)),
            dma((4, 6)), dma((4, 6)), dma((3,)), dma((3,)),
        ],
        compiler_params=pltpu.CompilerParams(
            collective_id=0, has_side_effects=True, vmem_limit_bytes=60 * 1024 * 1024
        ),
    )(normed, hidden, w_query, key_value_weight, w_out, q_gain, k_gain, ffn_gain, cosf, sinf, start)


def on_device(
    hidden,
    lengths,
    attn_gain,
    q_gain,
    key_norm_gain,
    w_query,
    key_value_weight,
    w_out,
    ffn_gain,
    w_router,
    routes,
    w_gate,
    w_up,
    w_down,
    page_table,
):
    column = lax.axis_index("exp")
    tokens_here = hidden.shape[0]
    model_width = hidden.shape[1]
    normed = rms_norm(hidden, attn_gain).astype(jnp.bfloat16)
    ends = jnp.cumsum(lengths[0])
    starts = ends - lengths[0]
    lane = jnp.arange(4, dtype=jnp.int32)[:, None]
    index = (lane * 4 + column % 4) * 128 + jnp.arange(128, dtype=jnp.int32)[None, :]
    inside = (index[..., None] >= starts) & (index[..., None] < ends)
    begin = jnp.sum(jnp.where(inside, starts, 0), -1)
    position = (index - begin).astype(jnp.float32)
    freqs = THETA_BASE ** (-jnp.arange(64, dtype=jnp.float32) * 2.0 / 128)
    angles = position[..., None] * freqs
    cosine, sine = jnp.cos(angles), jnp.sin(angles)
    cosf = jnp.concatenate([cosine, cosine], -1)
    sinf = jnp.concatenate([-sine, sine], -1)
    scale = math.log2(math.e) / math.sqrt(128)
    resid, moe_in, own_rows = attention_phase(
        normed, hidden, w_query, key_value_weight, w_out,
        (q_gain * scale).reshape(1, 128), key_norm_gain.reshape(1, 128),
        ffn_gain.reshape(1, 2048), cosf, sinf, begin[..., None],
    )
    logits = jnp.dot(moe_in, w_router, preferred_element_type=jnp.float32)
    soft_router = jax.nn.softmax(logits, -1)
    expert_count = w_router.shape[1]
    top_count = routes.shape[1]
    chosen = routes[:, :, None] == jnp.arange(expert_count, dtype=jnp.int32)[None, None, :]
    picked = jnp.sum(jnp.where(chosen, soft_router[:, None, :], 0.0), -1)
    gates = picked / jnp.sum(picked, 1, keepdims=True)
    capacity = 2 * tokens_here * top_count // expert_count
    flat_chosen = chosen.reshape(tokens_here * top_count, expert_count).astype(jnp.int32)
    ranks = jnp.cumsum(flat_chosen, 0) - 1
    slot_ids = jnp.sum(ranks * flat_chosen, 1)
    target = routes.reshape(-1) * capacity + slot_ids
    source_rows = moe_in[jnp.arange(tokens_here * top_count, dtype=jnp.int32) // top_count]
    send_rows = (
        jnp.zeros((expert_count * capacity, model_width), jnp.bfloat16).at[target].set(source_rows)
    )
    direct = send_rows.reshape(expert_count, capacity, model_width)
    batch = lax.all_to_all(direct, ("req", "exp"), split_axis=0, concat_axis=0, tiled=True)
    batch_shape = batch.shape
    rows_flat = batch.reshape(-1, batch_shape[-1])
    gate_part = jnp.dot(rows_flat, w_gate[0], preferred_element_type=jnp.float32)
    up_part = jnp.dot(rows_flat, w_up[0], preferred_element_type=jnp.float32)
    act = (jax.nn.silu(gate_part) * up_part).astype(jnp.bfloat16)
    answer = jnp.dot(act, w_down[0], preferred_element_type=jnp.float32).astype(jnp.bfloat16)
    answered = answer.reshape(batch_shape[:-1] + (w_down.shape[2],))
    returned = lax.all_to_all(answered, ("req", "exp"), split_axis=0, concat_axis=0, tiled=True)
    outcome = returned.reshape(expert_count * capacity, model_width)[target]
    outcome = outcome.reshape(tokens_here, top_count, model_width)
    moe_sum = jnp.sum(outcome.astype(jnp.float32) * gates[:, :, None], 1)
    layer_out = (resid.astype(jnp.float32) + moe_sum).astype(jnp.bfloat16)
    blocks_here = page_table.shape[0]
    page_size = tokens_here // blocks_here
    page_width = page_size * own_rows.shape[1]
    page_blocks = own_rows.reshape(blocks_here, page_width)
    req_count = lax.axis_size("req")
    per_peer = blocks_here // req_count
    owner = page_table // blocks_here // lax.axis_size("exp")
    owner_hit = (owner[:, None] == jnp.arange(req_count, dtype=jnp.int32)[None, :]).astype(
        jnp.int32
    )
    rank_inside = jnp.sum((jnp.cumsum(owner_hit, 0) - 1) * owner_hit, 1)
    send_order = owner * per_peer + rank_inside
    send_pages = jnp.zeros_like(page_blocks).at[send_order].set(page_blocks)
    send_slots = jnp.zeros_like(page_table).at[send_order].set(page_table % blocks_here)
    got_pages, got_slots = (
        lax.all_to_all(
            send_pages.reshape(req_count, per_peer, page_width),
            "req",
            split_axis=0,
            concat_axis=0,
            tiled=True,
        ),
        lax.all_to_all(
            send_slots.reshape(req_count, per_peer), "req", split_axis=0, concat_axis=0, tiled=True
        ),
    )
    kv_cache = (
        jnp.zeros_like(page_blocks)
        .at[got_slots.reshape(-1)]
        .set(got_pages.reshape(blocks_here, page_width))
    )
    return (layer_out, kv_cache)


def solution(mesh):
    in_specs = (
        P(("req", "exp"), None),
        P("req", None),
        P(),
        P(),
        P(),
        P(None, "exp"),
        P(),
        P("exp", None),
        P(),
        P(),
        P(("req", "exp"), None),
        P(("req", "exp"), None, None),
        P(("req", "exp"), None, None),
        P(("req", "exp"), None, None),
        P(("req", "exp")),
    )
    out_specs = (P(("req", "exp"), None), P(("req", "exp"), None))
    return jax.shard_map(
        on_device, mesh=mesh, in_specs=in_specs, out_specs=out_specs, check_vma=False
    )
```

time: 666 us -> 430 us (0.65)
  waiting for transfers between devices: 398 us -> 206 us
  Pallas kernels: 0 us -> 79.8 us
  matrix products: 106 us -> 33.3 us
  other arithmetic: 44.4 us -> 23.3 us
  local copies, waits for them, and re-layouts: 68 us -> 50.7 us
  between operations: 14.3 us -> 1.16 us
    all_gather x2 -> x0, waiting for transfers between devices: 115 us -> none  [the longest x1 68.8 us: on_device(): lax.all_gather(normed, 'exp', axis=0, tiled=True)]
    pallas_call x0 -> x1, Pallas kernels: none -> 79.8 us  [attention_phase(): pl.pallas_call(attention_kernel, name='attention', out_shape=(jax.ShapeDt...]
    reduce_scatter x1 -> x0, waiting for transfers between devices: 79.1 us -> none  [on_device(): lax.psum_scatter(jnp.dot(mixed, w_out, preferred_element_type=jnp.float32...]
    dot_general x7 -> x0, matrix products: 40.5 us -> none  [the longest x4 22.9 us: one_block(): jnp.einsum('hqk,kd->qhd', soft, values_in, preferred_element_type=jnp.flo...]
    sub x4 -> x0, matrix products: 31.5 us -> none  [one_block(): weights = jnp.exp(scores - highest)]
    and x4 -> x0, other arithmetic: 7.57 us -> none  [one_block(): (prompt_part[:, None] == prompt[None, :]) & (token_position[None, :] <= p...]
    dynamic_update_slice x8 -> x0, local copies, waits for them, and re-layouts: 7.25 us -> none  [attend(): lax.map(one_block, (query_blocks, prompt.reshape(block_list, block_rows),...]
    cos x2 -> x0, other arithmetic: 7.23 us -> none  [rotate(): cosine = jnp.cos(angles)[:, None, :]]
  transfers between devices with their start and end apart: 7 -> 4, of which waited for: 5 -> 2; matrix products, arithmetic and copies ran while one was open for 9% -> 11% of each run, Pallas kernels for 0% -> 0%
where the time goes in v1:
time: 430 us; the launch traced here: 423 us
  waiting for transfers between devices  206 us (48%)
  Pallas kernels  79.8 us (19%)
  local copies, waits for them, and re-layouts  50.7 us (12%)
  matrix products  33.3 us (8%)
  starting transfers between devices  29 us (7%)
  other arithmetic  23.3 us (5%)
    all_to_all x1, waiting for transfers between devices, on_device(): lax.all_to_all(answered, ('req', 'exp'), split_axis=0, concat_axis=0, til...  104 us
    all_to_all x1, waiting for transfers between devices, on_device(): lax.all_to_all(direct, ('req', 'exp'), split_axis=0, concat_axis=0, tiled...  101 us
    pallas_call x1, Pallas kernels, attention_phase(): pl.pallas_call(attention_kernel, name='attention', out_shape=(jax.ShapeDt...  79.8 us
    scatter x1, local copies, waits for them, and re-layouts, on_device(): jnp.zeros((expert_count * capacity, model_width), jnp.bfloat16).at[target]  25.7 us
    dot_general x1, matrix products, on_device(): jnp.dot(act, w_down[0], preferred_element_type=jnp.float32)  21.3 us
    gather x1, local copies, waits for them, and re-layouts, on_device(): outcome = returned.reshape(expert_count * capacity, model_width)[target]  13.7 us
    dot_general x1, matrix products, on_device(): jnp.dot(rows_flat, w_gate[0], preferred_element_type=jnp.float32)  11.7 us
    all_to_all x1, starting transfers between devices, on_device(): lax.all_to_all(answered, ('req', 'exp'), split_axis=0, concat_axis=0, til...  10.1 us
  transfers between devices with their start and end apart: 4, of which 2 were waited for; matrix products, arithmetic and copies ran while one was open for 11% of the time, Pallas kernels for 0%

profile of v1, /device:TPU:13, one launch (start us, length us, event | category | flops | bytes accessed | tf_op | source)
XLA Modules:
  0.0 422.8 jit_solution(3146286190460674195)
XLA Ops:
  0.7 0.8 broadcast_multiply_fusion
  1.5 0.9 copy.49
  2.6 0.8 reduce-window.14
  3.4 0.7 bitcast_subtract_fusion
  4.1 1.1 multiply_bitcast_fusion.q_gain
  5.2 1.2 fusion.10
  7.0 0.9 copy.47.start
  8.1 0.8 copy-done.2
  8.9 1.1 add_add_fusion
  10.5 2.0 fusion.12.normed
  12.5 1.0 fusion.23
  13.5 1.0 pad_maximum_fusion
  14.5 79.8 %attention.1 = (bf16[128,2048]{1,0:T(8,128)(2,1)}, bf16[128,2048]{1,0:T(8,128)(2,1)}, bf16[128,1024]{1,0:T(8,128)(2,1)}) custom-call(bf16[128,2048]{1,0:T(8,128)(2,1)} %fusion.12.normed, bf16[128,2048]{1,0:T(8,128)(2,1)} %hidden.1, bf16[2048,256]{1,0:T(8,128)(2,1)} %wq.1, bf16[2048,1024]{1,0:T(8,128)(2,1)} %kvw.1, bf16[256,2048]{1,0:T(8,128)(2,1)} %wo.1, ...), custom_call_target="tpu_custom_call" | custom-call | tf_op jit(solution)/shard_map/attention/pallas_call | solution.py:312
  94.3 25.7 %scatter_custom_fusion = bf16[2048,2048]{1,0:T(8,128)(2,1)} fusion(s32[1024]{0:T(1024)S(1)} %bitcast.60, bf16[128,2048]{1,0:T(8,128)(2,1)} %get-tuple-element.6, s32[1024]{0:T(1024)S(1)} %broadcast_clamp_fusion.1, bf16[]{:T(256)} %constant.106.clone.1), kind=kCustom, calls=%fused_computation.10 | custom fusion | bytes 8389120 | tf_op jit(solution)/shard_map/scatter | solution.py:398
  120.0 9.6 %all-to-all-start = ((bf16[128,16,2048]{2,1,0:T(8,128)(2,1)}), bf16[128,16,2048]{2,1,0:T(8,128)(2,1)}, u32[]{:S(2)}, u32[]{:S(2)}) async-start(bf16[128,16,2048]{2,1,0:T(8,128)(2,1)} %bitcast.55), calls=%async_computation | async-start | bytes 16777216 | tf_op jit(solution)/shard_map/all_to_all | solution.py:401
  130.5 0.7 copy.55
  131.2 0.8 reshape.327
  132.0 1.4 scatter_custom_fusion.2
  134.0 1.5 reduce.2
  135.5 1.8 reshape.354
  137.3 101.4 %all-to-all-done = bf16[128,16,2048]{2,1,0:T(8,128)(2,1)} async-done(((bf16[128,16,2048]{2,1,0:T(8,128)(2,1)}), bf16[128,16,2048]{2,1,0:T(8,128)(2,1)}, u32[]{:S(2)}, u32[]{:S(2)}) %all-to-all-start) | async-done | bytes 8388640 | tf_op jit(solution)/shard_map/all_to_all | solution.py:401
  238.8 4.3 %all-to-all-start.2 = ((s32[8,1,1]{2,1,0:T(1,128)}), s32[8,1,1]{2,1,0:T(1,128)S(1)}, u32[]{:S(2)}, u32[]{:S(2)}) async-start(s32[8,1,1]{2,1,0:T(1,128)} %copy.55), calls=%async_computation.2 | async-start | bytes 8192 | tf_op jit(solution)/shard_map/all_to_all | solution.py:436
  243.0 11.7 %fusion.7 = f32[2048,768]{1,0:T(8,128)} fusion(bf16[2048,2048]{1,0:T(8,128)(2,1)} %bitcast.14, bf16[1,2048,768]{2,1,0:T(8,128)(2,1)} %param.26), kind=kOutput, calls=%fused_computation.15 | convolution fusion | flops 6442450944 | bytes 17825792 | tf_op jit(solution)/shard_map/dot_general | solution.py:404
  254.7 5.0 %all-to-all-start.3 = ((bf16[8,2,8192]{2,1,0:T(2,128)(2,1)}), bf16[8,2,8192]{2,1,0:T(2,128)(2,1)S(1)}, u32[]{:S(2)}, u32[]{:S(2)}) async-start(bf16[8,2,8192]{2,1,0:T(2,128)(2,1)} %reshape.354), calls=%async_computation.3 | async-start | bytes 524288 | tf_op jit(solution)/shard_map/all_to_all | solution.py:429
  259.8 21.3 %convolution_convert_fusion = bf16[2048,2048]{1,0:T(8,128)(2,1)} fusion(f32[2048,768]{1,0:T(8,128)} %fusion.7, bf16[2048,2048]{1,0:T(8,128)(2,1)} %bitcast.14, bf16[1,768,2048]{2,1,0:T(8,128)(2,1)S(1)} %copy-done, bf16[1,2048,768]{2,1,0:T(8,128)(2,1)} %param.27), kind=kOutput, calls=%fused_computation.8 | convolution fusion | flops 12898533376 | bytes 29360128 | tf_op jit(solution)/shard_map/dot_general | solution.py:407
  281.1 10.1 %all-to-all-start.1 = ((bf16[128,16,2048]{2,1,0:T(8,128)(2,1)}), bf16[128,16,2048]{2,1,0:T(8,128)(2,1)}, u32[]{:S(2)}, u32[]{:S(2)}) async-start(bf16[128,16,2048]{2,1,0:T(8,128)(2,1)} %bitcast.56), calls=%async_computation.1 | async-start | bytes 16777216 | tf_op jit(solution)/shard_map/all_to_all | solution.py:409
  291.8 2.0 select_reduce_fusion
  294.4 1.9 scatter_custom_fusion.3
  296.3 104.1 %all-to-all-done.1 = bf16[128,16,2048]{2,1,0:T(8,128)(2,1)} async-done(((bf16[128,16,2048]{2,1,0:T(8,128)(2,1)}), bf16[128,16,2048]{2,1,0:T(8,128)(2,1)}, u32[]{:S(2)}, u32[]{:S(2)}) %all-to-all-start.1) | async-done | bytes 8388640 | tf_op jit(solution)/shard_map/all_to_all | solution.py:409
  400.4 13.7 %gather_fusion = bf16[1024,2048]{1,0:T(8,128)(2,1)} fusion(bf16[2048,2048]{1,0:T(8,128)(2,1)} %bitcast.19, s32[1024]{0:T(1024)S(1)} %broadcast_clamp_fusion), kind=kCustom, calls=%fused_computation.1 | custom fusion | bytes 8392704 | tf_op jit(solution)/shard_map/gather | solution.py:410
  414.1 6.5 %fusion = f32[128,2048]{1,0:T(8,128)S(1)} fusion(bf16[1024,2048]{1,0:T(8,128)(2,1)} %gather_fusion, f32[128,8]{1,0:T(8,128)S(1)} %broadcast_divide_fusion), kind=kLoop, calls=%fused_computation.7 | loop fusion | flops 6029312 | bytes 5246976 | tf_op jit(solution)/shard_map/reduce_sum | solution.py:412
  420.6 2.0 add_convert_fusion
  (51 shorter events, 4.0 us)
Async XLA Ops:
  0.6 259.2 %copy-start = (bf16[1,768,2048]{2,1,0:T(8,128)(2,1)S(1)}, bf16[1,768,2048]{2,1,0:T(8,128)(2,1)}, u32[]{:S(2)}) copy-start(bf16[1,768,2048]{2,1,0:T(8,128)(2,1)} %param.28) | copy-start | bytes 9437188
  8.1 0.8 copy-start.2
  120.0 9.6 %copy-start.6 = (s32[8]{0:T(128)S(1)}, s32[8]{0:T(128)}, u32[]{:S(2)}) copy-start(s32[8]{0:T(128)} %param.29) | copy-start | bytes 100
  120.0 11.2 %copy-start.5 = (bf16[128,1024]{1,0:T(8,128)(2,1)S(1)}, bf16[128,1024]{1,0:T(8,128)(2,1)}, u32[]{:S(2)}) copy-start(bf16[128,1024]{1,0:T(8,128)(2,1)} %get-tuple-element.7) | copy-start | bytes 786436
  120.0 118.7 %all-to-all-start = ((bf16[128,16,2048]{2,1,0:T(8,128)(2,1)}), bf16[128,16,2048]{2,1,0:T(8,128)(2,1)}, u32[]{:S(2)}, u32[]{:S(2)}) async-start(bf16[128,16,2048]{2,1,0:T(8,128)(2,1)} %bitcast.55), calls=%async_computation | async-start | bytes 16777216 | tf_op jit(solution)/shard_map/all_to_all | solution.py:401
  238.8 16.0 %all-to-all-start.2 = ((s32[8,1,1]{2,1,0:T(1,128)}), s32[8,1,1]{2,1,0:T(1,128)S(1)}, u32[]{:S(2)}, u32[]{:S(2)}) async-start(s32[8,1,1]{2,1,0:T(1,128)} %copy.55), calls=%async_computation.2 | async-start | bytes 8192 | tf_op jit(solution)/shard_map/all_to_all | solution.py:436
  254.7 26.3 %all-to-all-start.3 = ((bf16[8,2,8192]{2,1,0:T(2,128)(2,1)}), bf16[8,2,8192]{2,1,0:T(2,128)(2,1)S(1)}, u32[]{:S(2)}, u32[]{:S(2)}) async-start(bf16[8,2,8192]{2,1,0:T(2,128)(2,1)} %reshape.354), calls=%async_computation.3 | async-start | bytes 524288 | tf_op jit(solution)/shard_map/all_to_all | solution.py:429
  281.1 10.2 %copy-start.3 = (bf16[2048,128]{1,0:T(8,128)(2,1)S(1)}, bf16[2048,128]{1,0:T(8,128)(2,1)}, u32[]{:S(2)}) copy-start(bf16[2048,128]{1,0:T(8,128)(2,1)} %param.24) | copy-start | bytes 1572868
  281.1 10.2 %copy-start.4 = (bf16[128,2048]{1,0:T(8,128)(2,1)S(1)}, bf16[128,2048]{1,0:T(8,128)(2,1)}, u32[]{:S(2)}) copy-start(bf16[128,2048]{1,0:T(8,128)(2,1)} %get-tuple-element.6) | copy-start | bytes 1572868
  281.1 119.3 %all-to-all-start.1 = ((bf16[128,16,2048]{2,1,0:T(8,128)(2,1)}), bf16[128,16,2048]{2,1,0:T(8,128)(2,1)}, u32[]{:S(2)}, u32[]{:S(2)}) async-start(bf16[128,16,2048]{2,1,0:T(8,128)(2,1)} %bitcast.56), calls=%async_computation.1 | async-start | bytes 16777216 | tf_op jit(solution)/shard_map/all_to_all | solution.py:409
  400.4 22.2 %copy-start.1 = (bf16[1,768,2048]{2,1,0:T(8,128)(2,1)S(1)}, bf16[1,768,2048]{2,1,0:T(8,128)(2,1)}, u32[]{:S(2)}) copy-start(bf16[1,768,2048]{2,1,0:T(8,128)(2,1)} %param.28) | copy-start | bytes 9437188

commit v2 on v1

--- a/solution.py
+++ b/solution.py
@@ -385,18 +385,19 @@
     soft_router = jax.nn.softmax(logits, -1)
     expert_count = w_router.shape[1]
     top_count = routes.shape[1]
-    chosen = routes[:, :, None] == jnp.arange(expert_count, dtype=jnp.int32)[None, None, :]
-    picked = jnp.sum(jnp.where(chosen, soft_router[:, None, :], 0.0), -1)
-    gates = picked / jnp.sum(picked, 1, keepdims=True)
     capacity = 2 * tokens_here * top_count // expert_count
-    flat_chosen = chosen.reshape(tokens_here * top_count, expert_count).astype(jnp.int32)
-    ranks = jnp.cumsum(flat_chosen, 0) - 1
-    slot_ids = jnp.sum(ranks * flat_chosen, 1)
-    target = routes.reshape(-1) * capacity + slot_ids
-    source_rows = moe_in[jnp.arange(tokens_here * top_count, dtype=jnp.int32) // top_count]
-    send_rows = (
-        jnp.zeros((expert_count * capacity, model_width), jnp.bfloat16).at[target].set(source_rows)
-    )
+    experts = jnp.arange(expert_count, dtype=jnp.int32)
+    chosen = jnp.any(routes[:, None, :] == experts[None, :, None], -1)
+    weights = jnp.where(chosen, soft_router, 0.0)
+    gates = weights / jnp.sum(weights, 1, keepdims=True)
+    token = jnp.arange(tokens_here, dtype=jnp.int32)
+    earlier = (token[:, None] < token[None, :]).astype(BF)
+    chosen_t = chosen.T
+    ranks = jnp.dot(chosen_t.astype(BF), earlier, preferred_element_type=F32).astype(jnp.int32)
+    slot = jnp.arange(capacity, dtype=jnp.int32)
+    placed = chosen_t[:, None, :] & (ranks[:, None, :] == slot[None, :, None])
+    place = placed.astype(BF).reshape(expert_count * capacity, tokens_here)
+    send_rows = jnp.dot(place, moe_in, preferred_element_type=F32).astype(BF)
     direct = send_rows.reshape(expert_count, capacity, model_width)
     batch = lax.all_to_all(direct, ("req", "exp"), split_axis=0, concat_axis=0, tiled=True)
     batch_shape = batch.shape
@@ -407,9 +408,14 @@
     answer = jnp.dot(act, w_down[0], preferred_element_type=jnp.float32).astype(jnp.bfloat16)
     answered = answer.reshape(batch_shape[:-1] + (w_down.shape[2],))
     returned = lax.all_to_all(answered, ("req", "exp"), split_axis=0, concat_axis=0, tiled=True)
-    outcome = returned.reshape(expert_count * capacity, model_width)[target]
-    outcome = outcome.reshape(tokens_here, top_count, model_width)
-    moe_sum = jnp.sum(outcome.astype(jnp.float32) * gates[:, :, None], 1)
+    spread = jnp.where(placed, gates.T[:, None, :], 0.0).reshape(-1, tokens_here)
+    high = lax.reduce_precision(spread, 8, 7)
+    both = jnp.concatenate([high.astype(BF), (spread - high).astype(BF)], 1)
+    sums = lax.dot_general(
+        both, returned.reshape(-1, model_width), (((0,), (0,)), ((), ())),
+        preferred_element_type=F32,
+    )
+    moe_sum = sums[:tokens_here] + sums[tokens_here:]
     layer_out = (resid.astype(jnp.float32) + moe_sum).astype(jnp.bfloat16)
     blocks_here = page_table.shape[0]
     page_size = tokens_here // blocks_here

time: 430 us -> 387 us (0.900); the launches traced: 423 us -> 385 us
  local copies, waits for them, and re-layouts: 50.7 us -> 14.4 us
  matrix products: 33.3 us -> 47.4 us
  waiting for transfers between devices: 206 us -> 197 us
  other arithmetic: 23.3 us -> 17.4 us
    scatter x1 -> x0, local copies, waits for them, and re-layouts: 25.7 us -> none  [on_device(): jnp.zeros((expert_count * capacity, model_width), jnp.bfloat16).at[target]]
    gather x1 -> x0, local copies, waits for them, and re-layouts: 13.7 us -> none  [on_device(): outcome = returned.reshape(expert_count * capacity, model_width)[target]]
    dot_general x0 -> x3, matrix products: none -> 12.9 us  [the longest x1 6.59 us: on_device(): send_rows = jnp.dot(place, moe_in, preferred_element_type=F32).astype(BF)]
    all_to_all x1, waiting for transfers between devices: 104 us -> 96 us  [on_device(): lax.all_to_all(answered, ('req', 'exp'), split_axis=0, concat_axis=0, til...]
    reduce_sum x3 -> x1, other arithmetic: 8.89 us -> 1.27 us  [on_device(): gates = weights / jnp.sum(weights, 1, keepdims=True)]
  transfers between devices with their start and end apart: 4 -> 4, of which waited for: 2 -> 2; matrix products, arithmetic and copies ran while one was open for 11% -> 14% of each run, Pallas kernels for 0% -> 0%
where the time goes in v2:
time: 387 us; the launch traced here: 385 us
  waiting for transfers between devices  197 us (51%)
  Pallas kernels  79.8 us (21%)
  matrix products  47.4 us (12%)
  starting transfers between devices  28.3 us (7%)
  other arithmetic  17.4 us (4%)
  local copies, waits for them, and re-layouts  14.4 us (4%)
    all_to_all x1, waiting for transfers between devices, on_device(): lax.all_to_all(direct, ('req', 'exp'), split_axis=0, concat_axis=0, tiled...  101 us
    all_to_all x1, waiting for transfers between devices, on_device(): lax.all_to_all(answered, ('req', 'exp'), split_axis=0, concat_axis=0, til...  96 us
    pallas_call x1, Pallas kernels, attention_phase(): pl.pallas_call(attention_kernel, name='attention', out_shape=(jax.ShapeDt...  79.8 us
    dot_general x1, matrix products, on_device(): jnp.dot(act, w_down[0], preferred_element_type=jnp.float32)  21.3 us
    dot_general x1, matrix products, on_device(): jnp.dot(rows_flat, w_gate[0], preferred_element_type=jnp.float32)  11.7 us
    all_to_all x1, starting transfers between devices, on_device(): lax.all_to_all(answered, ('req', 'exp'), split_axis=0, concat_axis=0, til...  10.1 us
    all_to_all x1, starting transfers between devices, on_device(): lax.all_to_all(direct, ('req', 'exp'), split_axis=0, concat_axis=0, tiled...  9.09 us
  transfers between devices with their start and end apart: 4, of which 2 were waited for; matrix products, arithmetic and copies ran while one was open for 14% of the time, Pallas kernels for 0%

profile of v2, /device:TPU:13, one launch (start us, length us, event | category | flops | bytes accessed | tf_op | source)
XLA Modules:
  0.0 385.5 jit_solution(15298491591237175117)
XLA Ops:
  0.8 0.9 copy.45
  2.3 1.2 fusion.6
  3.6 1.1 multiply_bitcast_fusion.q_gain
  4.8 0.8 reduce-window.7
  6.4 0.9 copy.44.start
  7.3 2.0 fusion.8.normed
  9.3 1.0 fusion.24
  10.8 1.0 pad_maximum_fusion
  11.8 79.8 %attention.1 = (bf16[128,2048]{1,0:T(8,128)(2,1)}, bf16[128,2048]{1,0:T(8,128)(2,1)}, bf16[128,1024]{1,0:T(8,128)(2,1)}) custom-call(bf16[128,2048]{1,0:T(8,128)(2,1)} %fusion.8.normed, bf16[128,2048]{1,0:T(8,128)(2,1)} %hidden.1, bf16[2048,256]{1,0:T(8,128)(2,1)} %wq.1, bf16[2048,1024]{1,0:T(8,128)(2,1)} %kvw.1, bf16[256,2048]{1,0:T(8,128)(2,1)} %wo.1, ...), custom_call_target="tpu_custom_call" | custom-call | tf_op jit(solution)/shard_map/attention/pallas_call | solution.py:312
  91.6 6.6 %convolution_convert_fusion.1 = bf16[2048,2048]{1,0:T(8,128)(2,1)} fusion(pred[2048,128]{1,0:T(32,128)(4,1)S(1)} %fusion.16, bf16[128,2048]{1,0:T(8,128)(2,1)} %get-tuple-element.6), kind=kOutput, calls=%fused_computation.4 | convolution fusion | flops 1077936128 | bytes 9175040 | tf_op jit(solution)/shard_map/dot_general | solution.py:400
  98.2 9.1 %all-to-all-start = ((bf16[128,16,2048]{2,1,0:T(8,128)(2,1)}), bf16[128,16,2048]{2,1,0:T(8,128)(2,1)}, u32[]{:S(2)}, u32[]{:S(2)}) async-start(bf16[128,16,2048]{2,1,0:T(8,128)(2,1)} %bitcast.67), calls=%async_computation | async-start | bytes 16777216 | tf_op jit(solution)/shard_map/all_to_all | solution.py:402
  108.9 0.8 reshape.201
  109.7 1.6 scatter_custom_fusion.1
  111.9 1.5 reduce.1
  113.4 1.8 reshape.222
  115.2 101.3 %all-to-all-done = bf16[128,16,2048]{2,1,0:T(8,128)(2,1)} async-done(((bf16[128,16,2048]{2,1,0:T(8,128)(2,1)}), bf16[128,16,2048]{2,1,0:T(8,128)(2,1)}, u32[]{:S(2)}, u32[]{:S(2)}) %all-to-all-start) | async-done | bytes 8388640 | tf_op jit(solution)/shard_map/all_to_all | solution.py:402
  216.5 4.3 %all-to-all-start.2 = ((s32[8,1,1]{2,1,0:T(1,128)}), s32[8,1,1]{2,1,0:T(1,128)S(1)}, u32[]{:S(2)}, u32[]{:S(2)}) async-start(s32[8,1,1]{2,1,0:T(1,128)} %copy.50), calls=%async_computation.2 | async-start | bytes 8192 | tf_op jit(solution)/shard_map/all_to_all | solution.py:442
  220.7 11.7 %fusion.3 = f32[2048,768]{1,0:T(8,128)} fusion(bf16[2048,2048]{1,0:T(8,128)(2,1)} %bitcast.13, bf16[1,2048,768]{2,1,0:T(8,128)(2,1)} %param.26), kind=kOutput, calls=%fused_computation.8 | convolution fusion | flops 6442450944 | bytes 17825792 | tf_op jit(solution)/shard_map/dot_general | solution.py:405
  233.0 4.8 %all-to-all-start.3 = ((bf16[8,2,8192]{2,1,0:T(2,128)(2,1)}), bf16[8,2,8192]{2,1,0:T(2,128)(2,1)S(1)}, u32[]{:S(2)}, u32[]{:S(2)}) async-start(bf16[8,2,8192]{2,1,0:T(2,128)(2,1)} %reshape.222), calls=%async_computation.3 | async-start | bytes 524288 | tf_op jit(solution)/shard_map/all_to_all | solution.py:435
  237.8 21.3 %convolution_convert_fusion = bf16[2048,2048]{1,0:T(8,128)(2,1)} fusion(f32[2048,768]{1,0:T(8,128)} %fusion.3, bf16[2048,2048]{1,0:T(8,128)(2,1)} %bitcast.13, bf16[1,768,2048]{2,1,0:T(8,128)(2,1)S(1)} %copy-done, bf16[1,2048,768]{2,1,0:T(8,128)(2,1)} %param.27), kind=kOutput, calls=%fused_computation.3 | convolution fusion | flops 12898533376 | bytes 29360128 | tf_op jit(solution)/shard_map/dot_general | solution.py:408
  259.1 10.1 %all-to-all-start.1 = ((bf16[128,16,2048]{2,1,0:T(8,128)(2,1)}), bf16[128,16,2048]{2,1,0:T(8,128)(2,1)}, u32[]{:S(2)}, u32[]{:S(2)}) async-start(bf16[128,16,2048]{2,1,0:T(8,128)(2,1)} %bitcast.68), calls=%async_computation.1 | async-start | bytes 16777216 | tf_op jit(solution)/shard_map/all_to_all | solution.py:410
  270.0 1.6 fusion.35
  271.6 1.3 select_reduce_fusion
  273.6 1.6 fusion.25
  275.1 0.9 copy.49
  276.0 2.0 reduce-precision_convert_fusion
  278.1 0.9 reduce
  279.0 1.0 reshape.223
  280.0 2.4 scatter_custom_fusion.2
  282.4 96.0 %all-to-all-done.1 = bf16[128,16,2048]{2,1,0:T(8,128)(2,1)} async-done(((bf16[128,16,2048]{2,1,0:T(8,128)(2,1)}), bf16[128,16,2048]{2,1,0:T(8,128)(2,1)}, u32[]{:S(2)}, u32[]{:S(2)}) %all-to-all-start.1) | async-done | bytes 8388640 | tf_op jit(solution)/shard_map/all_to_all | solution.py:410
  378.4 6.1 %fusion.12 = f32[256,2048]{1,0:T(8,128)S(1)} fusion(bf16[2048,2048]{1,0:T(8,128)(2,1)} %bitcast.18, bf16[2048,128]{1,0:T(8,128)(2,1)} %get-tuple-element.11, bf16[2048,128]{1,0:T(8,128)(2,1)} %get-tuple-element.10), kind=kOutput, calls=%fused_computation.23 | convolution fusion | flops 2149580800 | bytes 11534336 | tf_op jit(solution)/shard_map/dot_general | solution.py:414
  384.5 1.0 fusion.11
  (41 shorter events, 6.3 us)
Async XLA Ops:
  0.6 237.2 %copy-start = (bf16[1,768,2048]{2,1,0:T(8,128)(2,1)S(1)}, bf16[1,768,2048]{2,1,0:T(8,128)(2,1)}, u32[]{:S(2)}) copy-start(bf16[1,768,2048]{2,1,0:T(8,128)(2,1)} %param.28) | copy-start | bytes 9437188
  0.8 90.9 %copy-start.4 = (s32[2048]{0:T(1024)}, s32[2048]{0:T(1024)S(1)}, u32[]{:S(2)}) copy-start(s32[2048]{0:T(1024)S(1)} %eq.57) | copy-start | bytes 24580
  2.3 95.9 %copy-start.3 = (pred[128,128]{1,0:T(8,128)(4,1)}, pred[128,128]{1,0:T(8,128)(4,1)S(1)}, u32[]{:S(2)}) copy-start(pred[128,128]{1,0:T(8,128)(4,1)S(1)} %copy.46) | copy-start | bytes 49156
  98.2 9.1 %copy-start.6 = (s32[8]{0:T(128)S(1)}, s32[8]{0:T(128)}, u32[]{:S(2)}) copy-start(s32[8]{0:T(128)} %param.29) | copy-start | bytes 100
  98.2 10.7 %copy-start.2 = (bf16[128,1024]{1,0:T(8,128)(2,1)S(1)}, bf16[128,1024]{1,0:T(8,128)(2,1)}, u32[]{:S(2)}) copy-start(bf16[128,1024]{1,0:T(8,128)(2,1)} %get-tuple-element.7) | copy-start | bytes 786436
  98.2 118.2 %all-to-all-start = ((bf16[128,16,2048]{2,1,0:T(8,128)(2,1)}), bf16[128,16,2048]{2,1,0:T(8,128)(2,1)}, u32[]{:S(2)}, u32[]{:S(2)}) async-start(bf16[128,16,2048]{2,1,0:T(8,128)(2,1)} %bitcast.67), calls=%async_computation | async-start | bytes 16777216 | tf_op jit(solution)/shard_map/all_to_all | solution.py:402
  216.5 16.0 %all-to-all-start.2 = ((s32[8,1,1]{2,1,0:T(1,128)}), s32[8,1,1]{2,1,0:T(1,128)S(1)}, u32[]{:S(2)}, u32[]{:S(2)}) async-start(s32[8,1,1]{2,1,0:T(1,128)} %copy.50), calls=%async_computation.2 | async-start | bytes 8192 | tf_op jit(solution)/shard_map/all_to_all | solution.py:442
  232.4 0.6 copy-start.5
  233.0 26.1 %all-to-all-start.3 = ((bf16[8,2,8192]{2,1,0:T(2,128)(2,1)}), bf16[8,2,8192]{2,1,0:T(2,128)(2,1)S(1)}, u32[]{:S(2)}, u32[]{:S(2)}) async-start(bf16[8,2,8192]{2,1,0:T(2,128)(2,1)} %reshape.222), calls=%async_computation.3 | async-start | bytes 524288 | tf_op jit(solution)/shard_map/all_to_all | solution.py:435
  259.1 119.3 %all-to-all-start.1 = ((bf16[128,16,2048]{2,1,0:T(8,128)(2,1)}), bf16[128,16,2048]{2,1,0:T(8,128)(2,1)}, u32[]{:S(2)}, u32[]{:S(2)}) async-start(bf16[128,16,2048]{2,1,0:T(8,128)(2,1)} %bitcast.68), calls=%async_computation.1 | async-start | bytes 16777216 | tf_op jit(solution)/shard_map/all_to_all | solution.py:410
  378.4 6.1 %copy-start.1 = (bf16[128,2048]{1,0:T(8,128)(2,1)S(1)}, bf16[128,2048]{1,0:T(8,128)(2,1)}, u32[]{:S(2)}) copy-start(bf16[128,2048]{1,0:T(8,128)(2,1)} %get-tuple-element.5) | copy-start | bytes 1572868

commit v3 on v2

--- a/solution.py
+++ b/solution.py
@@ -340,6 +340,193 @@
             collective_id=0, has_side_effects=True, vmem_limit_bytes=60 * 1024 * 1024
         ),
     )(normed, hidden, w_query, key_value_weight, w_out, q_gain, k_gain, ffn_gain, cosf, sinf, start)
+
+
+def offset_parts(i):
+    chunk = lax.div(i, 16)
+    inner = lax.rem(i, 16)
+    oy, oz = lax.div(inner, 4), lax.rem(inner, 4)
+    ox = lax.rem(lax.rem(chunk, 4) + 8 - oy - oz, 4)
+    return oy, lax.div(chunk, 4), oz, ox
+
+
+def experts_kernel(
+    moe, resid, place, place_t, chosen, router, wg, wu, wd,
+    out,
+    rows, batch, answers, back, wgv, wuv, wdv, acc,
+    lsem, dsend, drecv, asend, arecv,
+):
+    req = lax.axis_index("req")
+    col = lax.axis_index("exp")
+    y, core = lax.div(req, 2), lax.rem(req, 2)
+    z, x = lax.div(col, 4), lax.rem(col, 4)
+
+    def target(i):
+        oy, oc, oz, ox = offset_parts(i)
+        return (
+            lax.rem(y + oy, 4) * 2 + core + oc - 2 * core * oc,
+            lax.rem(z + oz, 4) * 4 + lax.rem(x + ox, 4),
+        )
+
+    def origin(i):
+        oy, oc, oz, ox = offset_parts(i)
+        return (
+            lax.rem(y + 4 - oy, 4) * 2 + core + oc - 2 * core * oc,
+            lax.rem(z + 4 - oz, 4) * 4 + lax.rem(x + 4 - ox, 4),
+        )
+
+    loads = [
+        pltpu.make_async_copy(src.at[0], dst, lsem.at[n])
+        for n, (src, dst) in enumerate(((wg, wgv), (wu, wuv), (wd, wdv)))
+    ]
+    for c in loads:
+        c.start()
+
+    barrier = pltpu.get_barrier_semaphore()
+
+    def greet(i, carry):
+        pl.semaphore_signal(barrier, inc=1, device_id=target(i), device_id_type=MESH)
+        return carry
+
+    lax.fori_loop(1, 128, greet, 0)
+
+    def chunk_rows(j):
+        return pl.ds(pl.multiple_of(j * 256, 256), 256)
+
+    def build(j, carry):
+        r = chunk_rows(j)
+        rows[r, :] = jnp.dot(place[r, :], moe[...], preferred_element_type=F32).astype(BF)
+        return carry
+
+    lax.fori_loop(0, 8, build, 0)
+    batch[0:16, :] = rows[0:16, :]
+    pl.semaphore_wait(barrier, 127)
+
+    def dispatch(i, carry):
+        r = pl.ds(pl.multiple_of(i * 16, 16), 16)
+        pltpu.make_async_remote_copy(
+            src_ref=rows.at[r], dst_ref=batch.at[r],
+            send_sem=dsend.at[lax.div(i, 16)], recv_sem=drecv.at[lax.div(i, 16)],
+            device_id=target(i), device_id_type=MESH,
+        ).start()
+        return carry
+
+    lax.fori_loop(1, 128, dispatch, 0)
+
+    def whole(buf, ssem, rsem, j, r):
+        return pltpu.make_async_remote_copy(
+            src_ref=buf.at[r], dst_ref=buf.at[r], send_sem=ssem.at[j], recv_sem=rsem.at[j],
+            device_id=target(1), device_id_type=MESH,
+        )
+
+    def arrived(buf, ssem, rsem, j):
+        @pl.when(j == 0)
+        def _():
+            whole(buf, ssem, rsem, j, pl.ds(16, 240)).wait_recv()
+
+        @pl.when(j > 0)
+        def _():
+            whole(buf, ssem, rsem, j, chunk_rows(j)).wait_recv()
+
+    def left(buf, ssem, rsem, j):
+        @pl.when(j == 0)
+        def _():
+            whole(buf, ssem, rsem, j, pl.ds(16, 240)).wait_send()
+
+        @pl.when(j > 0)
+        def _():
+            whole(buf, ssem, rsem, j, chunk_rows(j)).wait_send()
+
+    logits = jnp.dot(moe[...], router[...], preferred_element_type=F32)
+    grown = jnp.exp(logits - jnp.max(logits, -1, keepdims=True))
+    soft = grown / jnp.sum(grown, -1, keepdims=True)
+    picked = soft * chosen[...]
+    gates = picked / jnp.sum(picked, -1, keepdims=True)
+    high = gates.astype(BF)
+    low = (gates - high.astype(F32)).astype(BF)
+    both = jnp.concatenate([high, low], 0)
+    acc[...] = jnp.zeros((256, 2048), F32)
+    for c in loads:
+        c.wait()
+
+    def work(j, carry):
+        arrived(batch, dsend, drecv, j)
+        r = chunk_rows(j)
+        taken = batch[r, :]
+        g = jnp.dot(taken, wgv[...], preferred_element_type=F32)
+        u = jnp.dot(taken, wuv[...], preferred_element_type=F32)
+        act = (g / (1.0 + jnp.exp(-g)) * u).astype(BF)
+        answers[r, :] = jnp.dot(act, wdv[...], preferred_element_type=F32).astype(BF)
+
+        def reply(q, inner):
+            i = j * 16 + q
+            p = pl.ds(pl.multiple_of(i * 16, 16), 16)
+            pltpu.make_async_remote_copy(
+                src_ref=answers.at[p], dst_ref=back.at[p],
+                send_sem=asend.at[j], recv_sem=arecv.at[j],
+                device_id=origin(i), device_id_type=MESH,
+            ).start()
+            return inner
+
+        @pl.when(j == 0)
+        def _():
+            back[0:16, :] = answers[0:16, :]
+            lax.fori_loop(1, 16, reply, 0)
+
+        @pl.when(j > 0)
+        def _():
+            lax.fori_loop(0, 16, reply, 0)
+
+        return carry
+
+    lax.fori_loop(0, 8, work, 0)
+
+    def combine(j, carry):
+        arrived(back, asend, arecv, j)
+        r = chunk_rows(j)
+        expert = lax.broadcasted_iota(jnp.int32, (128, 256), 0)
+        owner = j * 16 + lax.broadcasted_iota(jnp.int32, (128, 256), 1) // 16
+        pick = jnp.where(expert == owner, 1.0, 0.0).astype(BF)
+        spread = jnp.dot(both, pick, preferred_element_type=F32)
+        mask = place_t[:, r].astype(F32)
+        spread = (spread.reshape(2, 128, 256) * mask[None]).reshape(256, 256).astype(BF)
+        acc[...] += jnp.dot(spread, back[r, :], preferred_element_type=F32)
+        return carry
+
+    lax.fori_loop(0, 8, combine, 0)
+    out[...] = (resid[...].astype(F32) + (acc[0:128, :] + acc[128:256, :])).astype(BF)
+
+    def drain(j, carry):
+        left(rows, dsend, drecv, j)
+        left(answers, asend, arecv, j)
+        return carry
+
+    lax.fori_loop(0, 8, drain, 0)
+
+
+def expert_phase(moe_in, resid, place, place_t, chosen, router, w_gate, w_up, w_down):
+    vmem = pl.BlockSpec(memory_space=pltpu.VMEM)
+    hbm = pl.BlockSpec(memory_space=pl.ANY)
+    dma = pltpu.SemaphoreType.DMA
+    slots = pltpu.VMEM((2048, 2048), BF)
+    return pl.pallas_call(
+        experts_kernel,
+        name="experts",
+        out_shape=jax.ShapeDtypeStruct((128, 2048), BF),
+        in_specs=[vmem] * 6 + [hbm] * 3,
+        out_specs=vmem,
+        scratch_shapes=[
+            slots, slots, slots, slots,
+            pltpu.VMEM((2048, 768), BF),
+            pltpu.VMEM((2048, 768), BF),
+            pltpu.VMEM((768, 2048), BF),
+            pltpu.VMEM((256, 2048), F32),
+            dma((3,)), dma((8,)), dma((8,)), dma((8,)), dma((8,)),
+        ],
+        compiler_params=pltpu.CompilerParams(
+            collective_id=1, has_side_effects=True, vmem_limit_bytes=60 * 1024 * 1024
+        ),
+    )(moe_in, resid, place, place_t, chosen, router, w_gate, w_up, w_down)
 
 
 def on_device(
@@ -381,15 +568,14 @@
         (q_gain * scale).reshape(1, 128), key_norm_gain.reshape(1, 128),
         ffn_gain.reshape(1, 2048), cosf, sinf, begin[..., None],
     )
-    logits = jnp.dot(moe_in, w_router, preferred_element_type=jnp.float32)
-    soft_router = jax.nn.softmax(logits, -1)
     expert_count = w_router.shape[1]
     top_count = routes.shape[1]
     capacity = 2 * tokens_here * top_count // expert_count
-    experts = jnp.arange(expert_count, dtype=jnp.int32)
+    req = lax.axis_index("req")
+    oy, oc, oz, ox = offset_parts(jnp.arange(expert_count, dtype=jnp.int32))
+    to_req = (req // 2 + oy) % 4 * 2 + (req % 2 + oc) % 2
+    experts = to_req * 16 + (column // 4 + oz) % 4 * 4 + (column % 4 + ox) % 4
     chosen = jnp.any(routes[:, None, :] == experts[None, :, None], -1)
-    weights = jnp.where(chosen, soft_router, 0.0)
-    gates = weights / jnp.sum(weights, 1, keepdims=True)
     token = jnp.arange(tokens_here, dtype=jnp.int32)
     earlier = (token[:, None] < token[None, :]).astype(BF)
     chosen_t = chosen.T
@@ -397,26 +583,11 @@
     slot = jnp.arange(capacity, dtype=jnp.int32)
     placed = chosen_t[:, None, :] & (ranks[:, None, :] == slot[None, :, None])
     place = placed.astype(BF).reshape(expert_count * capacity, tokens_here)
-    send_rows = jnp.dot(place, moe_in, preferred_element_type=F32).astype(BF)
-    direct = send_rows.reshape(expert_count, capacity, model_width)
-    batch = lax.all_to_all(direct, ("req", "exp"), split_axis=0, concat_axis=0, tiled=True)
-    batch_shape = batch.shape
-    rows_flat = batch.reshape(-1, batch_shape[-1])
-    gate_part = jnp.dot(rows_flat, w_gate[0], preferred_element_type=jnp.float32)
-    up_part = jnp.dot(rows_flat, w_up[0], preferred_element_type=jnp.float32)
-    act = (jax.nn.silu(gate_part) * up_part).astype(jnp.bfloat16)
-    answer = jnp.dot(act, w_down[0], preferred_element_type=jnp.float32).astype(jnp.bfloat16)
-    answered = answer.reshape(batch_shape[:-1] + (w_down.shape[2],))
-    returned = lax.all_to_all(answered, ("req", "exp"), split_axis=0, concat_axis=0, tiled=True)
-    spread = jnp.where(placed, gates.T[:, None, :], 0.0).reshape(-1, tokens_here)
-    high = lax.reduce_precision(spread, 8, 7)
-    both = jnp.concatenate([high.astype(BF), (spread - high).astype(BF)], 1)
-    sums = lax.dot_general(
-        both, returned.reshape(-1, model_width), (((0,), (0,)), ((), ())),
-        preferred_element_type=F32,
-    )
-    moe_sum = sums[:tokens_here] + sums[tokens_here:]
-    layer_out = (resid.astype(jnp.float32) + moe_sum).astype(jnp.bfloat16)
+    order = (experts[None, :] == jnp.arange(expert_count, dtype=jnp.int32)[:, None]).astype(BF)
+    router = jnp.dot(w_router, order, preferred_element_type=F32).astype(BF)
+    layer_out = expert_phase(
+        moe_in, resid, place, place.T, chosen.astype(F32), router, w_gate, w_up, w_down
+    )
     blocks_here = page_table.shape[0]
     page_size = tokens_here // blocks_here
     page_width = page_size * own_rows.shape[1]

time: 387 us -> 354 us (0.915); the launches traced: 385 us -> 347 us
  Pallas kernels: 79.8 us -> 312 us
  waiting for transfers between devices: 197 us -> 0.01 us
  matrix products: 47.4 us -> 1.32 us
  starting transfers between devices: 28.3 us -> 10.1 us
  other arithmetic: 17.4 us -> 10.4 us
    pallas_call x0 -> x1, Pallas kernels: none -> 232 us  [expert_phase(): pl.pallas_call(experts_kernel, name='experts', out_shape=jax.ShapeDtypeSt...]
    all_to_all x2 -> x0, waiting for transfers between devices: 197 us -> none  [the longest x1 101 us: on_device(): lax.all_to_all(direct, ('req', 'exp'), split_axis=0, concat_axis=0, tiled...]
    dot_general x5 -> x1, matrix products: 47.2 us -> 1.11 us  [on_device(): router = jnp.dot(w_router, order, preferred_element_type=F32).astype(BF)]
    all_to_all x2 -> x0, starting transfers between devices: 19.2 us -> none  [the longest x1 10.1 us: on_device(): lax.all_to_all(answered, ('req', 'exp'), split_axis=0, concat_axis=0, til...]
  transfers between devices with their start and end apart: 4 -> 2, of which waited for: 2 -> 0; matrix products, arithmetic and copies ran while one was open for 14% -> 5% of each run, Pallas kernels for 0% -> 90%
where the time goes in v3:
time: 354 us; the launch traced here: 347 us
  Pallas kernels  312 us (88%)
  local copies, waits for them, and re-layouts  12.8 us (4%)
  other arithmetic  10.4 us (3%)
  starting transfers between devices  10.1 us (3%)
    pallas_call x1, Pallas kernels, expert_phase(): pl.pallas_call(experts_kernel, name='experts', out_shape=jax.ShapeDtypeSt...  232 us
    pallas_call x1, Pallas kernels, attention_phase(): pl.pallas_call(attention_kernel, name='attention', out_shape=(jax.ShapeDt...  80.2 us
  transfers between devices with their start and end apart: 2, of which 0 were waited for; matrix products, arithmetic and copies ran while one was open for 5% of the time, Pallas kernels for 90%

profile of v3, /device:TPU:13, one launch (start us, length us, event | category | flops | bytes accessed | tf_op | source)
XLA Modules:
  0.0 347.4 jit_solution(11594408259702584338)
XLA Ops:
  0.7 0.8 and_select_fusion
  1.7 0.6 scatter_custom_fusion
  2.3 0.7 copy.53
  3.0 5.2 %all-to-all-start = ((s32[8,1,1]{2,1,0:T(1,128)}), s32[8,1,1]{2,1,0:T(1,128)S(1)}, u32[]{:S(2)}, u32[]{:S(2)}) async-start(s32[8,1,1]{2,1,0:T(1,128)} %copy.53), calls=%async_computation | async-start | bytes 8192 | tf_op jit(solution)/shard_map/all_to_all | solution.py:613
  8.3 1.2 fusion.1
  9.5 1.2 multiply_bitcast_fusion.q_gain
  10.8 0.8 reduce-window.7
  11.7 0.7 bitcast_subtract_fusion
  12.5 0.9 copy.46.start
  13.3 0.8 copy.47
  14.2 0.3 compare_reduce_fusion
  14.4 0.2 convolution_convert_fusion.1
  14.9 0.4 copy.50
  15.4 0.3 copy.49
  15.8 1.0 fusion.3.normed
  16.8 1.0 fusion.10
  17.8 1.0 pad_maximum_fusion
  18.8 80.2 %attention.1 = (bf16[128,2048]{1,0:T(8,128)(2,1)}, bf16[128,2048]{1,0:T(8,128)(2,1)}, bf16[128,1024]{1,0:T(8,128)(2,1)}) custom-call(bf16[128,2048]{1,0:T(8,128)(2,1)} %fusion.3.normed, bf16[128,2048]{1,0:T(8,128)(2,1)} %hidden.1, bf16[2048,256]{1,0:T(8,128)(2,1)} %wq.1, bf16[2048,1024]{1,0:T(8,128)(2,1)} %kvw.1, bf16[256,2048]{1,0:T(8,128)(2,1)} %wo.1, ...), custom_call_target="tpu_custom_call" | custom-call | tf_op jit(solution)/shard_map/attention/pallas_call | solution.py:312
  99.0 1.1 reshape.350
  100.0 1.2 scatter_custom_fusion.1
  101.3 0.5 broadcast.509
  101.8 0.8 reduce.1
  102.6 0.9 reshape.371
  103.7 4.8 %all-to-all-start.1 = ((bf16[8,2,8192]{2,1,0:T(2,128)(2,1)}), bf16[8,2,8192]{2,1,0:T(2,128)(2,1)S(1)}, u32[]{:S(2)}, u32[]{:S(2)}) async-start(bf16[8,2,8192]{2,1,0:T(2,128)(2,1)} %reshape.371), calls=%async_computation.1 | async-start | bytes 524288 | tf_op jit(solution)/shard_map/all_to_all | solution.py:606
  108.5 1.1 fusion.router
  109.6 0.6 convert_element_type.39.chosen
  110.3 1.0 copy.52.place
  111.3 231.8 %experts.1 = bf16[128,2048]{1,0:T(8,128)(2,1)} custom-call(bf16[128,2048]{1,0:T(8,128)(2,1)} %get-tuple-element.5.moe, bf16[128,2048]{1,0:T(8,128)(2,1)} %get-tuple-element.6.resid, bf16[2048,128]{1,0:T(8,128)(2,1)} %copy.52.place, bf16[128,2048]{1,0:T(8,128)(2,1)} %bitcast.27, f32[128,128]{1,0:T(8,128)} %convert_element_type.39.chosen, ...), custom_call_target="tpu_custom_call" | custom-call | tf_op jit(solution)/shard_map/experts/pallas_call | solution.py:512
  343.1 0.2 reduce
  343.4 0.3 reshape.372
  343.6 1.9 scatter_custom_fusion.2
  345.5 1.9 copy.63
  (28 shorter events, 1.2 us)
Async XLA Ops:
  0.6 107.9 %copy-start = (bf16[2048,128]{1,0:T(8,128)(2,1)S(1)}, bf16[2048,128]{1,0:T(8,128)(2,1)}, u32[]{:S(2)}) copy-start(bf16[2048,128]{1,0:T(8,128)(2,1)} %param.24) | copy-start | bytes 1572868
  0.6 15.1 %copy-start.2 = (bf16[128,2048]{1,0:T(8,128)(2,1)S(1)}, bf16[128,2048]{1,0:T(8,128)(2,1)}, u32[]{:S(2)}) copy-start(bf16[128,2048]{1,0:T(8,128)(2,1)} %hidden.1) | copy-start | bytes 1572868
  0.7 15.1 %copy-start.3 = (f32[2048]{0:T(1024)S(1)}, f32[2048]{0:T(1024)}, u32[]{:S(2)}) copy-start(f32[2048]{0:T(1024)} %param.17) | copy-start | bytes 24580
  3.0 100.7 %all-to-all-start = ((s32[8,1,1]{2,1,0:T(1,128)}), s32[8,1,1]{2,1,0:T(1,128)S(1)}, u32[]{:S(2)}, u32[]{:S(2)}) async-start(s32[8,1,1]{2,1,0:T(1,128)} %copy.53), calls=%async_computation | async-start | bytes 8192 | tf_op jit(solution)/shard_map/all_to_all | solution.py:613
  103.7 7.6 %copy-start.1 = (bf16[2048,128]{0,1:T(8,128)(2,1)}, bf16[2048,128]{0,1:T(8,128)(2,1)S(1)}, u32[]{:S(2)}) copy-start(bf16[2048,128]{0,1:T(8,128)(2,1)S(1)} %and_convert_fusion) | copy-start | bytes 1572868
  103.7 239.7 %all-to-all-start.1 = ((bf16[8,2,8192]{2,1,0:T(2,128)(2,1)}), bf16[8,2,8192]{2,1,0:T(2,128)(2,1)S(1)}, u32[]{:S(2)}, u32[]{:S(2)}) async-start(bf16[8,2,8192]{2,1,0:T(2,128)(2,1)} %reshape.371), calls=%async_computation.1 | async-start | bytes 524288 | tf_op jit(solution)/shard_map/all_to_all | solution.py:606

commit v4 on v3

--- a/solution.py
+++ b/solution.py
@@ -351,10 +351,11 @@
 
 
 def experts_kernel(
-    moe, resid, place, place_t, chosen, router, wg, wu, wd,
-    out,
+    moe, resid, place, place_t, chosen, router, own, turn, goal, wg, wu, wd,
+    out, cache,
     rows, batch, answers, back, wgv, wuv, wdv, acc,
-    lsem, dsend, drecv, asend, arecv,
+    pages, got_pages, got_goal,
+    lsem, dsend, drecv, asend, arecv, psend, precv, gsend, grecv,
 ):
     req = lax.axis_index("req")
     col = lax.axis_index("exp")
@@ -400,7 +401,31 @@
 
     lax.fori_loop(0, 8, build, 0)
     batch[0:16, :] = rows[0:16, :]
+
+    pages[...] = jnp.dot(turn[...], own[...], preferred_element_type=F32).astype(BF)
+
+    def page(r):
+        return pl.ds(pl.multiple_of(r * 16, 16), 16)
+
+    got_pages[page(req), :] = pages[page(req), :]
+    got_goal[page(req), :] = goal[page(req), :]
     pl.semaphore_wait(barrier, 127)
+
+    def page_copies(d, there, here):
+        dev = (lax.rem(req + d, 8), col)
+        return [
+            pltpu.make_async_remote_copy(
+                src_ref=src.at[page(there)], dst_ref=dst.at[page(here)],
+                send_sem=ssem.at[d], recv_sem=rsem.at[d], device_id=dev, device_id_type=MESH,
+            )
+            for src, dst, ssem, rsem in (
+                (pages, got_pages, psend, precv), (goal, got_goal, gsend, grecv)
+            )
+        ]
+
+    for d in range(1, 8):
+        for c in page_copies(d, lax.rem(req + d, 8), req):
+            c.start()
 
     def dispatch(i, carry):
         r = pl.ds(pl.multiple_of(i * 16, 16), 16)
@@ -481,6 +506,13 @@
 
     lax.fori_loop(0, 8, work, 0)
 
+    for d in range(1, 8):
+        for c in page_copies(d, lax.rem(req + d, 8), lax.rem(req + 8 - d, 8)):
+            c.wait_recv()
+    at = lax.broadcasted_iota(jnp.int32, (128, 128), 1)
+    settle = jnp.where(got_goal[...] == at, 1.0, 0.0).T.astype(BF)
+    cache[...] = jnp.dot(settle, got_pages[...], preferred_element_type=F32).astype(BF)
+
     def combine(j, carry):
         arrived(back, asend, arecv, j)
         r = chunk_rows(j)
@@ -502,9 +534,12 @@
         return carry
 
     lax.fori_loop(0, 8, drain, 0)
-
-
-def expert_phase(moe_in, resid, place, place_t, chosen, router, w_gate, w_up, w_down):
+    for d in range(1, 8):
+        for c in page_copies(d, lax.rem(req + d, 8), req):
+            c.wait_send()
+
+
+def expert_phase(moe_in, resid, place, place_t, chosen, router, own, turn, goal, w_gate, w_up, w_down):
     vmem = pl.BlockSpec(memory_space=pltpu.VMEM)
     hbm = pl.BlockSpec(memory_space=pl.ANY)
     dma = pltpu.SemaphoreType.DMA
@@ -512,21 +547,28 @@
     return pl.pallas_call(
         experts_kernel,
         name="experts",
-        out_shape=jax.ShapeDtypeStruct((128, 2048), BF),
-        in_specs=[vmem] * 6 + [hbm] * 3,
-        out_specs=vmem,
+        out_shape=(
+            jax.ShapeDtypeStruct((128, 2048), BF),
+            jax.ShapeDtypeStruct((128, 1024), BF),
+        ),
+        in_specs=[vmem] * 9 + [hbm] * 3,
+        out_specs=(vmem, vmem),
         scratch_shapes=[
             slots, slots, slots, slots,
             pltpu.VMEM((2048, 768), BF),
             pltpu.VMEM((2048, 768), BF),
             pltpu.VMEM((768, 2048), BF),
             pltpu.VMEM((256, 2048), F32),
+            pltpu.VMEM((128, 1024), BF),
+            pltpu.VMEM((128, 1024), BF),
+            pltpu.VMEM((128, 128), jnp.int32),
             dma((3,)), dma((8,)), dma((8,)), dma((8,)), dma((8,)),
+            dma((8,)), dma((8,)), dma((8,)), dma((8,)),
         ],
         compiler_params=pltpu.CompilerParams(
             collective_id=1, has_side_effects=True, vmem_limit_bytes=60 * 1024 * 1024
         ),
-    )(moe_in, resid, place, place_t, chosen, router, w_gate, w_up, w_down)
+    )(moe_in, resid, place, place_t, chosen, router, own, turn, goal, w_gate, w_up, w_down)
 
 
 def on_device(
@@ -585,40 +627,20 @@
     place = placed.astype(BF).reshape(expert_count * capacity, tokens_here)
     order = (experts[None, :] == jnp.arange(expert_count, dtype=jnp.int32)[:, None]).astype(BF)
     router = jnp.dot(w_router, order, preferred_element_type=F32).astype(BF)
-    layer_out = expert_phase(
-        moe_in, resid, place, place.T, chosen.astype(F32), router, w_gate, w_up, w_down
-    )
     blocks_here = page_table.shape[0]
     page_size = tokens_here // blocks_here
-    page_width = page_size * own_rows.shape[1]
-    page_blocks = own_rows.reshape(blocks_here, page_width)
-    req_count = lax.axis_size("req")
-    per_peer = blocks_here // req_count
     owner = page_table // blocks_here // lax.axis_size("exp")
-    owner_hit = (owner[:, None] == jnp.arange(req_count, dtype=jnp.int32)[None, :]).astype(
-        jnp.int32
+    peer, inside_page = token // page_size, token % page_size
+    from_block = owner[None, :] == jnp.arange(blocks_here, dtype=jnp.int32)[:, None]
+    spot = jnp.sum(jnp.where(from_block, page_table % blocks_here, 0), 1)
+    same = inside_page[:, None] == inside_page[None, :]
+    turn = (jnp.repeat(owner, page_size)[None, :] == peer[:, None]) & same
+    goal = jnp.repeat(spot, page_size) * page_size + inside_page
+    layer_out, cache_rows = expert_phase(
+        moe_in, resid, place, place.T, chosen.astype(F32), router, own_rows, turn.astype(BF),
+        jnp.broadcast_to(goal[:, None], (tokens_here, 128)), w_gate, w_up, w_down,
     )
-    rank_inside = jnp.sum((jnp.cumsum(owner_hit, 0) - 1) * owner_hit, 1)
-    send_order = owner * per_peer + rank_inside
-    send_pages = jnp.zeros_like(page_blocks).at[send_order].set(page_blocks)
-    send_slots = jnp.zeros_like(page_table).at[send_order].set(page_table % blocks_here)
-    got_pages, got_slots = (
-        lax.all_to_all(
-            send_pages.reshape(req_count, per_peer, page_width),
-            "req",
-            split_axis=0,
-            concat_axis=0,
-            tiled=True,
-        ),
-        lax.all_to_all(
-            send_slots.reshape(req_count, per_peer), "req", split_axis=0, concat_axis=0, tiled=True
-        ),
-    )
-    kv_cache = (
-        jnp.zeros_like(page_blocks)
-        .at[got_slots.reshape(-1)]
-        .set(got_pages.reshape(blocks_here, page_width))
-    )
+    kv_cache = cache_rows.reshape(blocks_here, page_size * own_rows.shape[1])
     return (layer_out, kv_cache)
 
 

time: 354 us -> 341 us (0.963); the launches traced: 347 us -> 341 us
  Pallas kernels: 312 us -> 324 us
  starting transfers between devices: 10.1 us -> 0 us
  local copies, waits for them, and re-layouts: 12.8 us -> 8.49 us
  other arithmetic: 10.4 us -> 6.18 us
    pallas_call x1, Pallas kernels: 232 us -> 244 us  [expert_phase(): pl.pallas_call(experts_kernel, name='experts', out_shape=(jax.ShapeDtypeS...]
    all_to_all x2 -> x0, starting transfers between devices: 10.1 us -> none  [the longest x1 5.23 us: on_device(): lax.all_to_all(send_slots.reshape(req_count, per_peer), 'req', split_axis...]
    scatter x3 -> x0, local copies, waits for them, and re-layouts: 3.69 us -> none  [the longest x1 1.89 us: on_device(): kv_cache = jnp.zeros_like(page_blocks).at[got_slots.reshape(-1)].set(got_...]
  transfers between devices with their start and end apart: 2 -> 0, of which waited for: 0 -> 0; matrix products, arithmetic and copies ran while one was open for 5% -> 0% of each run, Pallas kernels for 90% -> 0%
where the time goes in v4:
time: 341 us
  Pallas kernels  324 us (95%)
  local copies, waits for them, and re-layouts  8.49 us (2%)
  other arithmetic  6.18 us (2%)
    pallas_call x1, Pallas kernels, expert_phase(): pl.pallas_call(experts_kernel, name='experts', out_shape=(jax.ShapeDtypeS...  244 us
    pallas_call x1, Pallas kernels, attention_phase(): pl.pallas_call(attention_kernel, name='attention', out_shape=(jax.ShapeDt...  79.8 us

profile of v4, /device:TPU:13, one launch (start us, length us, event | category | flops | bytes accessed | tf_op | source)
XLA Modules:
  0.0 340.5 jit_solution(8858560303820196934)
XLA Ops:
  0.7 0.8 copy.29
  1.5 0.3 compare_reduce_fusion
  1.8 0.2 convolution_convert_fusion.1
  2.1 0.3 copy.31
  2.5 0.1 copy.30
  2.6 0.1 and.212
  2.7 0.4 copy.32
  3.1 0.1 eq.103
  3.2 0.2 and_convert_fusion
  3.4 1.0 copy.34.place
  4.4 0.1 iota_add_fusion
  4.5 0.2 reduce-window.7
  4.7 0.1 select_reduce_fusion
  4.8 0.1 subtract_convert_fusion
  4.9 1.0 fusion.4
  5.9 1.0 pad_maximum_fusion
  6.9 0.9 copy.28.start
  7.7 0.2 fusion.1
  7.9 1.0 fusion.3.normed
  8.9 0.6 multiply_bitcast_fusion.q_gain
  9.5 79.8 %attention.1 = (bf16[128,2048]{1,0:T(8,128)(2,1)}, bf16[128,2048]{1,0:T(8,128)(2,1)}, bf16[128,1024]{1,0:T(8,128)(2,1)}) custom-call(bf16[128,2048]{1,0:T(8,128)(2,1)} %fusion.3.normed, bf16[128,2048]{1,0:T(8,128)(2,1)} %hidden.1, bf16[2048,256]{1,0:T(8,128)(2,1)} %wq.1, bf16[2048,1024]{1,0:T(8,128)(2,1)} %kvw.1, bf16[256,2048]{1,0:T(8,128)(2,1)} %wo.1, ...), custom_call_target="tpu_custom_call" | custom-call | tf_op jit(solution)/shard_map/attention/pallas_call | solution.py:312
  89.4 1.1 fusion.router
  90.5 0.6 convert_element_type.39.chosen
  91.1 0.1 broadcast_in_dim.19
  91.2 0.1 eq.108
  91.3 0.7 and_convert_fusion.1.turn
  92.0 0.1 select_reduce_fusion.1
  92.2 0.1 mul.118
  92.3 0.7 broadcast_in_dim.23.goal
  93.0 243.9 %experts.1 = (bf16[128,2048]{1,0:T(8,128)(2,1)}, bf16[128,1024]{1,0:T(8,128)(2,1)}) custom-call(bf16[128,2048]{1,0:T(8,128)(2,1)} %get-tuple-element.7.moe, bf16[128,2048]{1,0:T(8,128)(2,1)} %get-tuple-element.8.resid, bf16[2048,128]{1,0:T(8,128)(2,1)} %copy.34.place, bf16[128,2048]{1,0:T(8,128)(2,1)} %bitcast.18, f32[128,128]{1,0:T(8,128)} %convert_element_type.39.chosen, ...), custom_call_target="tpu_custom_call" | custom-call | tf_op jit(solution)/shard_map/experts/pallas_call | solution.py:547
  336.8 1.8 reshape.342
  338.6 1.9 copy.37
  (26 shorter events, 0.3 us)
Async XLA Ops:
  0.6 88.7 %copy-start = (bf16[2048,128]{1,0:T(8,128)(2,1)S(1)}, bf16[2048,128]{1,0:T(8,128)(2,1)}, u32[]{:S(2)}) copy-start(bf16[2048,128]{1,0:T(8,128)(2,1)} %param.24) | copy-start | bytes 1572868
  2.1 2.4 copy-start.4
  2.5 5.3 %copy-start.2 = (bf16[128,2048]{1,0:T(8,128)(2,1)S(1)}, bf16[128,2048]{1,0:T(8,128)(2,1)}, u32[]{:S(2)}) copy-start(bf16[128,2048]{1,0:T(8,128)(2,1)} %hidden.1) | copy-start | bytes 1572868
  2.7 5.3 %copy-start.3 = (f32[2048]{0:T(1024)S(1)}, f32[2048]{0:T(1024)}, u32[]{:S(2)}) copy-start(f32[2048]{0:T(1024)} %param.17) | copy-start | bytes 24580
  3.2 5.7 %copy-start.5 = (f32[128]{0:T(128)S(1)}, f32[128]{0:T(128)}, u32[]{:S(2)}) copy-start(f32[128]{0:T(128)} %param.18) | copy-start | bytes 1540
  3.4 85.9 %copy-start.1 = (bf16[2048,128]{0,1:T(8,128)(2,1)}, bf16[2048,128]{0,1:T(8,128)(2,1)S(1)}, u32[]{:S(2)}) copy-start(bf16[2048,128]{0,1:T(8,128)(2,1)S(1)} %and_convert_fusion) | copy-start | bytes 1572868
  9.5 81.6 %copy-start.6 = (s32[8]{0:T(128)S(1)}, s32[8]{0:T(128)}, u32[]{:S(2)}) copy-start(s32[8]{0:T(128)} %param.29) | copy-start | bytes 100
